TPU v7x, 256 devices: a whole 4x4x8 slice. The times are simulated.
256 devices in a mesh: wide: 64 (over z_lo, x, y), narrow: 4 (over z_hi, core).
Axes of the slice: x: 4, y: 4, z: 8 (z_hi: 2, z_lo: 4; z = z_hi * 4 + z_lo), core: 2. Of those that a mesh axis runs over, the one named last changes fastest.
Arguments:
- constraint_mats: bfloat16 [1024, 256, 256], P(('narrow', 'wide')), may hold values from -0.375 to 0.375
- primal_matrix: bfloat16 [256, 256], replicated, may hold values from -0.25 to 0.25
- inverse_dual_iterate: bfloat16 [256, 256], replicated, may hold values from -0.25 to 0.25
Outputs:
- schur: float32 [1024, 1024], P(('narrow', 'wide'))
All inputs are finite; a program needn't handle non-finite values.
Results may differ from a plain program's by a relative error of at most 0.0029.
Values may be sent and summed in bfloat16 or wider, within the bound.
A program may use at most 64 MiB of HBM per device.

v0:
```python
import jax
import jax.numpy as jnp
from jax import lax
from jax.sharding import PartitionSpec as P


def contract(u_rows, constraint_row_stack):
    return lax.dot_general(
        u_rows, constraint_row_stack, (((1,), (1,)), ((), ())), preferred_element_type=jnp.float32
    )


def body(constraint_mats, primal_matrix, inverse_dual_iterate):
    count = constraint_mats.shape[0]
    order = constraint_mats.shape[1]
    left_product = jnp.einsum(
        "ab,ibc->iac", primal_matrix, constraint_mats, preferred_element_type=jnp.float32
    ).astype(jnp.bfloat16)
    product_matrices = jnp.einsum(
        "lsx,xm->lsm", left_product, inverse_dual_iterate, preferred_element_type=jnp.float32
    ).astype(jnp.bfloat16)
    u_flat = product_matrices.reshape(count, order * order)
    a_flat = constraint_mats.reshape(count, order * order)
    product_pieces, a_slices = (
        lax.all_to_all(u_flat, "wide", split_axis=1, concat_axis=0, tiled=True),
        lax.all_to_all(a_flat, "wide", split_axis=1, concat_axis=0, tiled=True),
    )
    u_every, a_every = (
        lax.all_gather(product_pieces, "narrow", axis=0, tiled=True),
        lax.all_gather(a_slices, "narrow", axis=0, tiled=True),
    )
    partial_value = 0.5 * (contract(product_pieces, a_every) + contract(a_slices, u_every))
    schur = lax.psum_scatter(partial_value, "wide", scatter_dimension=0, tiled=True)
    return schur


def solution(mesh):
    in_specs = (P(("narrow", "wide"), None, None), P(), P())
    out_specs = P(("narrow", "wide"), None)
    return jax.shard_map(body, mesh=mesh, in_specs=in_specs, out_specs=out_specs, check_vma=False)
```

profile of v0, /device:TPU:8, one launch (start us, length us, event | category | flops | bytes accessed | tf_op | source)
XLA Modules:
  0.0 844.7 jit_solution(17084348686302862161)
XLA Ops:
  6.5 0.0 copy-start
  6.5 0.0 all-gather.3.cloned.1.call-start
  6.5 1.4 all_to_all.32
  7.9 0.0 copy-start.2
  7.9 0.0 copy-start.3
  8.0 0.4 copy.11
  8.4 28.8 %all_to_all.38 = bf16[4,64,1024]{2,0,1:T(4,128)(2,1)S(1)} all-to-all(bf16[4,64,1024]{2,0,1:T(4,128)(2,1)S(1)} %copy.11), channel_id=1, replica_groups=mesh['wide'=64,'narrow'=4] {'wide'}, dimensions={1} | all-to-all | bytes 1048576 | tf_op jit(solution)/shard_map/all_to_all | solution.py:26
  37.2 0.9 all_to_all.35
  38.1 0.0 all-gather.3.cloned.1.call-update
  38.1 0.0 all-gather.5.cloned.1.call-start
  38.2 0.0 copy-done
  38.2 0.0 copy-done.2
  38.2 0.0 copy-done.3
  38.2 0.8 convolution_convert_fusion
  39.0 0.3 all_to_all.28
  39.3 0.4 copy.10
  39.8 44.4 %all_to_all.39 = bf16[4,64,1024]{2,0,1:T(4,128)(2,1)S(1)} all-to-all(bf16[4,64,1024]{2,0,1:T(4,128)(2,1)S(1)} %copy.10), channel_id=1, replica_groups=mesh['wide'=64,'narrow'=4] {'wide'}, dimensions={1} | all-to-all | bytes 1048576 | tf_op jit(solution)/shard_map/all_to_all | solution.py:25
  84.2 0.9 all_to_all.31
  85.1 0.0 copy-start.1
  85.1 0.0 all-gather.5.cloned.1.call-update
  85.1 0.0 all-reduce.3.cloned.1.call-start
  85.2 0.0 all-gather.3.cloned.1.call-done
  85.2 2.5 fusion.6
  87.7 0.0 copy-start.4
  87.8 38.3 %all-gather.5.cloned.1.call-done = bf16[1024,1024]{1,0:T(8,128)(2,1)} async-done(((bf16[256,1024]{1,0:T(8,128)(2,1)}), bf16[1024,1024]{1,0:T(8,128)(2,1)}) %all-gather.5.cloned.1.call-update) | async-done | bytes 2097168 | tf_op jit(solution)/shard_map/all_gather | solution.py:29
  126.0 0.0 copy-done.1
  126.0 3.3 fusion.1
  129.3 0.0 all-reduce.3.cloned.1.call-update
  129.4 0.0 copy-done.4
  129.4 0.6 dynamic-slice
  130.6 706.2 %all-reduce.3.cloned.1.call-done = f32[256,1024]{1,0:T(8,128)} async-done(((f32[256,1024]{1,0:T(8,128)}), f32[256,1024]{1,0:T(8,128)}) %all-reduce.3.cloned.1.call-update) | async-done | bytes 1048592
  836.8 1.4 constant_dynamic-slice_fusion
Async XLA Ops:
  6.5 31.7 %copy-start = (bf16[256,256]{1,0:T(8,128)(2,1)S(1)}, bf16[256,256]{1,0:T(8,128)(2,1)}, u32[]{:S(2)}) copy-start(bf16[256,256]{1,0:T(8,128)(2,1)} %param.5) | copy-start | bytes 393220
  6.5 78.6 %all-gather.3.cloned.1.call-start = ((), (), s32[]{:S(2)}) async-start(), calls=%async_computation.2 | async-start | bytes 2621440 | tf_op jit(solution)/shard_map/all_gather | solution.py:30
  7.9 30.3 %copy-start.2 = (bf16[4,256,256]{2,1,0:T(8,128)(2,1)S(1)}, bf16[4,256,256]{2,1,0:T(8,128)(2,1)}, u32[]{:S(2)}) copy-start(bf16[4,256,256]{2,1,0:T(8,128)(2,1)} %param.3) | copy-start | bytes 1572868
  7.9 30.3 %copy-start.3 = (bf16[256,256]{1,0:T(8,128)(2,1)S(1)}, bf16[256,256]{1,0:T(8,128)(2,1)}, u32[]{:S(2)}) copy-start(bf16[256,256]{1,0:T(8,128)(2,1)} %param.4) | copy-start | bytes 393220
  38.1 87.9 %all-gather.5.cloned.1.call-start = ((), (), s32[]{:S(2)}) async-start(), calls=%async_computation.3 | async-start | bytes 2621440 | tf_op jit(solution)/shard_map/all_gather | solution.py:29
  85.1 40.9 %copy-start.1 = (bf16[256,1024]{1,0:T(8,128)(2,1)S(1)}, bf16[256,1024]{1,0:T(8,128)(2,1)}, u32[]{:S(2)}) copy-start(bf16[256,1024]{1,0:T(8,128)(2,1)} %all_to_all.35) | copy-start | bytes 1572868
  85.1 751.7 %all-reduce.3.cloned.1.call-start = ((), (), s32[]{:S(2)}) async-start(), calls=%async_computation.4 | async-start | bytes 2097152
  87.7 41.6 %copy-start.4 = (u32[256]{0:T(256)S(1)}, u32[256]{0:T(256)}, u32[]{:S(2)}) copy-start(u32[256]{0:T(256)} %constant.5) | copy-start | bytes 3076
Sparse Core Ops, SparseCore 0:
  38.3 42.0 all-gather.2
  85.2 40.7 all-gather.4
  129.5 707.3 all-reduce.2
where the time goes:
time: 845 us
  waiting for transfers between devices  745 us (88%)
  blocking collectives  73.2 us (9%)
  between operations  13.9 us (2%)
    unnamed x4, waiting for transfers between devices  706 us
    all_to_all x1, blocking collectives, body(): lax.all_to_all(u_flat, 'wide', split_axis=1, concat_axis=0, tiled=True)  44.4 us
    all_gather x1, waiting for transfers between devices, body(): lax.all_gather(product_pieces, 'narrow', axis=0, tiled=True)  38.3 us
    all_to_all x1, blocking collectives, body(): lax.all_to_all(a_flat, 'wide', split_axis=1, concat_axis=0, tiled=True)  28.8 us
  transfers between devices with their start and end apart: 3, of which 2 were waited for; matrix products, arithmetic and copies ran while one was open for 1% of the time, Pallas kernels for 0%

commit v1 on v0

v1 whole, which is shorter than its diff:
```python
import jax
import jax.numpy as jnp
from jax import lax
from jax.experimental import pallas as pl
from jax.experimental.pallas import tpu as pltpu
from jax.sharding import PartitionSpec as P

PARTS = 16
LINE = 4
COUNT = 4
ROWS = 16
LANES = 128
SLICE = 2 * COUNT * ROWS + 2 * COUNT
DEPTH = (ROWS + 1) * LANES
GROUP = PARTS * COUNT


def dot(a, b):
    return lax.dot_general(a, b, (((1,), (0,)), ((), ())), preferred_element_type=jnp.float32)


def dot_nt(a, b):
    return lax.dot_general(a, b, (((1,), (1,)), ((), ())), preferred_element_type=jnp.float32)


def kernel(a_ref, x_ref, z_ref, out_ref, send1, recv1, wide_rows, diag_rows, v_all, a_own, a_all, partial, send3, recv3,
           send4, recv4, joined, s1, r1, s2v, r2v, s2a, r2a, s3, r3, s4, r4, own_sem):
    wide, narrow = lax.axis_index("wide"), lax.axis_index("narrow")
    y = lax.rem(wide, 4)
    x = lax.rem(lax.div(wide, 4), 4)
    z_lo = lax.div(wide, 16)
    part = narrow * 4 + z_lo

    def in_column(p):
        return {"wide": lax.rem(p, 4) * 16 + x * 4 + y, "narrow": lax.div(p, 4)}

    def along_x(k):
        return {"wide": z_lo * 16 + k * 4 + y, "narrow": narrow}

    def along_y(k):
        return {"wide": z_lo * 16 + x * 4 + k, "narrow": narrow}

    barrier = pltpu.get_barrier_semaphore()
    for k in range(1, PARTS):
        pl.semaphore_signal(barrier, inc=1, device_id=in_column(lax.rem(part + k, PARTS)))
    for k in range(1, LINE):
        pl.semaphore_signal(barrier, inc=1, device_id=along_x(lax.rem(x + k, LINE)))
        pl.semaphore_signal(barrier, inc=1, device_id=along_y(lax.rem(y + k, LINE)))

    row = lax.broadcasted_iota(jnp.int32, (LANES, LANES), 0)
    col = lax.broadcasted_iota(jnp.int32, (LANES, LANES), 1)
    primal, dual = x_ref[...], z_ref[...]
    diag_a, diag_v = [], []
    for c in range(COUNT):
        mat = a_ref[c]
        left = dot(primal, mat).astype(jnp.bfloat16)
        top = dot(left[:LANES], dual) + dot_nt(dual[:LANES], left)
        low = dot(left[LANES:], dual[:, LANES:]) + dot_nt(dual[LANES:], left[LANES:])
        mat32 = mat.astype(jnp.float32)
        a_up, a_low = mat32[:LANES, :LANES], mat32[LANES:, LANES:]
        fold_a = [mat[:LANES, LANES:], jnp.where(row <= col, a_up, a_low).astype(jnp.bfloat16)]
        corner = jnp.where(row < col, top[:, :LANES], jnp.where(row == col, 0.5 * top[:, :LANES], low))
        fold_v = [top[:, LANES:].astype(jnp.bfloat16), corner.astype(jnp.bfloat16)]
        diag_a.append(jnp.sum(jnp.where(row == col, a_low, 0.0), axis=0, keepdims=True))
        diag_v.append(jnp.sum(jnp.where(row == col, low, 0.0), axis=0, keepdims=True) * (0.5 / PARTS))
        for d in range(PARTS):
            half, at = d // 8, (d % 8) * ROWS
            send1[d, ROWS * c:ROWS * (c + 1), :] = fold_a[half][at:at + ROWS]
            send1[d, ROWS * (COUNT + c):ROWS * (COUNT + c + 1), :] = fold_v[half][at:at + ROWS]
    diag = jnp.concatenate(diag_a + diag_v, axis=0).astype(jnp.bfloat16)
    for d in range(PARTS):
        send1[d, 2 * COUNT * ROWS:, :] = diag

    pl.semaphore_wait(barrier, PARTS - 1 + 2 * (LINE - 1))

    def copy1(slot, to):
        return pltpu.make_async_remote_copy(
            src_ref=send1.at[to], dst_ref=recv1.at[slot], send_sem=s1.at[to], recv_sem=r1.at[slot], device_id=in_column(to)
        )

    for k in range(1, PARTS):
        copy1(part, lax.rem(part + k, PARTS)).start()
    own = pltpu.make_async_copy(send1.at[part], recv1.at[part], own_sem)
    own.start()
    own.wait()
    for k in range(1, PARTS):
        src = lax.rem(part + k, PARTS)
        copy1(src, src).wait_recv()

    for s in range(PARTS):
        block = recv1[s].astype(jnp.float32)
        wide_rows[0, GROUP * s:GROUP * (s + 1), :] = block[:GROUP]
        wide_rows[1, GROUP * s:GROUP * (s + 1), :] = block[GROUP:2 * GROUP]
        diag_rows[0, COUNT * s:COUNT * (s + 1), :] = block[2 * GROUP:2 * GROUP + COUNT]
        diag_rows[1, COUNT * s:COUNT * (s + 1), :] = block[2 * GROUP + COUNT:]
    for r in range(ROWS):
        at = pl.ds(r * LANES, LANES)
        part_a = wide_rows[0, pl.ds(r, GROUP, stride=ROWS), :].astype(jnp.bfloat16)
        for n in range(LINE):
            a_own[n, :, at] = part_a[ROWS * n:ROWS * (n + 1)]
        v_all[y, :, at] = wide_rows[1, pl.ds(r, GROUP, stride=ROWS), :].astype(jnp.bfloat16)
    at = pl.ds(ROWS * LANES, LANES)
    part_a = diag_rows[0].astype(jnp.bfloat16)
    for n in range(LINE):
        a_own[n, :, at] = part_a[ROWS * n:ROWS * (n + 1)]
    v_all[y, :, at] = diag_rows[1].astype(jnp.bfloat16)

    def copy_v(slot, to):
        return pltpu.make_async_remote_copy(
            src_ref=v_all.at[slot], dst_ref=v_all.at[slot], send_sem=s2v.at[to], recv_sem=r2v.at[slot], device_id=along_y(to)
        )

    def copy_a(slot, to):
        return pltpu.make_async_remote_copy(
            src_ref=a_own, dst_ref=a_all.at[:, slot], send_sem=s2a.at[to], recv_sem=r2a.at[slot], device_id=along_x(to)
        )

    for k in (2, 1, 3):
        copy_v(y, lax.rem(y + k, LINE)).start()
        copy_a(x, lax.rem(x + k, LINE)).start()
    own = pltpu.make_async_copy(a_own, a_all.at[:, x], own_sem)
    own.start()
    own.wait()
    for k in (1, 3, 2):
        src = lax.rem(y + k, LINE)
        copy_v(src, src).wait_recv()
        src = lax.rem(x + k, LINE)
        copy_a(src, src).wait_recv()

    partial[...] = dot_nt(
        v_all[...].reshape(LINE * GROUP, DEPTH), a_all[...].reshape(LINE * GROUP, DEPTH)
    )
    for p in range(PARTS):
        for k in range(LINE):
            send3[p, COUNT * k:COUNT * (k + 1), :] = partial[GROUP * k + COUNT * p:GROUP * k + COUNT * (p + 1), :]

    def copy3(slot, to):
        return pltpu.make_async_remote_copy(
            src_ref=send3.at[to], dst_ref=recv3.at[slot], send_sem=s3.at[to], recv_sem=r3.at[slot], device_id=in_column(to)
        )

    for k in range(1, PARTS):
        copy3(part, lax.rem(part + k, PARTS)).start()
    total = send3[part]
    for k in range(1, PARTS):
        src = lax.rem(part + k, PARTS)
        copy3(src, src).wait_recv()
        total = total + recv3[src]
    for k in range(LINE):
        send4[k] = total[COUNT * k:COUNT * (k + 1)]

    def copy4(slot, to):
        return pltpu.make_async_remote_copy(
            src_ref=send4.at[to], dst_ref=recv4.at[slot], send_sem=s4.at[to], recv_sem=r4.at[slot], device_id=along_y(to)
        )

    for k in range(1, LINE):
        copy4(y, lax.rem(y + k, LINE)).start()
    recv4[y] = send4[y]
    for k in range(1, LINE):
        src = lax.rem(y + k, LINE)
        copy4(src, src).wait_recv()

    for k in range(LINE):
        piece = recv4[k]
        for n in range(LINE):
            joined[COUNT * n:COUNT * (n + 1), GROUP * k:GROUP * (k + 1)] = piece[:, GROUP * n:GROUP * (n + 1)]
    wide_row = lax.broadcasted_iota(jnp.int32, (4 * GROUP, 4 * GROUP), 0)
    wide_col = lax.broadcasted_iota(jnp.int32, (4 * GROUP, 4 * GROUP), 1)
    digit = lambda v, size: lax.rem(lax.div(v, size), 4)
    source = digit(wide_col, 4) * 64 + digit(wide_col, 16) * 16 + digit(wide_col, 64) * 4 + digit(wide_col, 1)
    pick = jnp.where(wide_row == source, 1.0, 0.0).astype(jnp.bfloat16)
    value = joined[...]
    high = value.astype(jnp.bfloat16)
    rest = value - high.astype(jnp.float32)
    mid = rest.astype(jnp.bfloat16)
    low = (rest - mid.astype(jnp.float32)).astype(jnp.bfloat16)
    ordered = dot(high, pick) + dot(mid, pick) + dot(low, pick)
    for n in range(LINE):
        out_ref[:, 4 * GROUP * n:4 * GROUP * (n + 1)] = ordered[COUNT * n:COUNT * (n + 1)]

    for k in range(1, PARTS):
        to = lax.rem(part + k, PARTS)
        copy1(part, to).wait_send()
        copy3(part, to).wait_send()
    for k in range(1, LINE):
        to = lax.rem(y + k, LINE)
        copy_v(y, to).wait_send()
        copy4(y, to).wait_send()
        copy_a(x, lax.rem(x + k, LINE)).wait_send()


def body(constraint_mats, primal_matrix, inverse_dual_iterate):
    vmem = pl.BlockSpec(memory_space=pltpu.VMEM)
    dma = pltpu.SemaphoreType.DMA
    bf16, f32 = jnp.bfloat16, jnp.float32
    return pl.pallas_call(
        kernel,
        out_shape=jax.ShapeDtypeStruct((COUNT, 1024), f32),
        in_specs=[vmem] * 3,
        out_specs=vmem,
        scratch_shapes=[
            pltpu.VMEM((PARTS, SLICE, LANES), bf16),
            pltpu.VMEM((PARTS, SLICE, LANES), bf16),
            pltpu.VMEM((2, PARTS * GROUP, LANES), f32),
            pltpu.VMEM((2, GROUP, LANES), f32),
            pltpu.VMEM((LINE, GROUP, DEPTH), bf16),
            pltpu.VMEM((LINE, ROWS, DEPTH), bf16),
            pltpu.VMEM((LINE, LINE, ROWS, DEPTH), bf16),
            pltpu.VMEM((LINE * GROUP, LINE * GROUP), f32),
            pltpu.VMEM((PARTS, LINE * COUNT, LINE * GROUP), f32),
            pltpu.VMEM((PARTS, LINE * COUNT, LINE * GROUP), f32),
            pltpu.VMEM((LINE, COUNT, LINE * GROUP), f32),
            pltpu.VMEM((LINE, COUNT, LINE * GROUP), f32),
            pltpu.VMEM((LINE * COUNT, LINE * GROUP), f32),
            dma((PARTS,)), dma((PARTS,)),
            dma((LINE,)), dma((LINE,)), dma((LINE,)), dma((LINE,)),
            dma((PARTS,)), dma((PARTS,)),
            dma((LINE,)), dma((LINE,)),
            dma,
        ],
        compiler_params=pltpu.CompilerParams(collective_id=0, has_side_effects=True, vmem_limit_bytes=32 << 20),
        name="schur",
    )(constraint_mats, primal_matrix, inverse_dual_iterate)


def solution(mesh):
    in_specs = (P(("narrow", "wide"), None, None), P(), P())
    out_specs = P(("narrow", "wide"), None)
    return jax.shard_map(body, mesh=mesh, in_specs=in_specs, out_specs=out_specs, check_vma=False)
```

time: 845 us -> 57 us (0.07)
  the two profiles are of different devices: /device:TPU:8 before, /device:TPU:1 now
where the time goes in v1:
time: 57 us; the launch traced here: 56.8 us
  Pallas kernels  53.4 us (94%)
  local copies, waits for them, and re-layouts  3.46 us (6%)
    pallas_call x1, Pallas kernels, body(): pl.pallas_call(kernel, out_shape=jax.ShapeDtypeStruct((COUNT, 1024), f32)...  53.4 us
    unnamed x7, local copies, waits for them, and re-layouts  3.46 us

profile of v1, /device:TPU:1, one launch (start us, length us, event | category | flops | bytes accessed | tf_op | source)
XLA Modules:
  0.0 56.8 jit_solution(18101984176176703457)
XLA Ops:
  0.0 0.0 copy-start
  0.0 1.0 %copy-done = bf16[4,256,256]{2,1,0:T(8,128)(2,1)S(1)} copy-done((bf16[4,256,256]{2,1,0:T(8,128)(2,1)S(1)}, bf16[4,256,256]{2,1,0:T(8,128)(2,1)}, u32[]{:S(2)}) %copy-start) | copy-done | bytes 524312
  1.0 0.0 copy-start.1
  1.0 0.9 %copy-done.1 = bf16[256,256]{1,0:T(8,128)(2,1)S(1)} copy-done((bf16[256,256]{1,0:T(8,128)(2,1)S(1)}, bf16[256,256]{1,0:T(8,128)(2,1)}, u32[]{:S(2)}) %copy-start.1) | copy-done | bytes 131096
  1.9 0.0 copy-start.2
  1.9 0.9 %copy-done.2 = bf16[256,256]{1,0:T(8,128)(2,1)S(1)} copy-done((bf16[256,256]{1,0:T(8,128)(2,1)S(1)}, bf16[256,256]{1,0:T(8,128)(2,1)}, u32[]{:S(2)}) %copy-start.2) | copy-done | bytes 131096
  2.9 53.4 %schur.1 = f32[4,1024]{1,0:T(4,128)S(1)} custom-call(bf16[4,256,256]{2,1,0:T(8,128)(2,1)S(1)} %copy-done, bf16[256,256]{1,0:T(8,128)(2,1)S(1)} %copy-done.1, bf16[256,256]{1,0:T(8,128)(2,1)S(1)} %copy-done.2), custom_call_target="tpu_custom_call" | custom-call | tf_op jit(solution)/shard_map/schur/pallas_call | solution.py:197
  56.2 0.6 %copy.5 = f32[4,1024]{1,0:T(4,128)} copy(f32[4,1024]{1,0:T(4,128)S(1)} %schur.1) | data formatting | bytes 32768
Async XLA Ops:
  0.0 1.0 %copy-start = (bf16[4,256,256]{2,1,0:T(8,128)(2,1)S(1)}, bf16[4,256,256]{2,1,0:T(8,128)(2,1)}, u32[]{:S(2)}) copy-start(bf16[4,256,256]{2,1,0:T(8,128)(2,1)} %a_ref.1) | copy-start | bytes 1572868
  1.0 0.9 %copy-start.1 = (bf16[256,256]{1,0:T(8,128)(2,1)S(1)}, bf16[256,256]{1,0:T(8,128)(2,1)}, u32[]{:S(2)}) copy-start(bf16[256,256]{1,0:T(8,128)(2,1)} %x_ref.1) | copy-start | bytes 393220
  1.9 0.9 %copy-start.2 = (bf16[256,256]{1,0:T(8,128)(2,1)S(1)}, bf16[256,256]{1,0:T(8,128)(2,1)}, u32[]{:S(2)}) copy-start(bf16[256,256]{1,0:T(8,128)(2,1)} %z_ref.1) | copy-start | bytes 393220

commit v2 on v0

v2 whole, which is shorter than its diff:
```python
import jax
import jax.numpy as jnp
from jax import lax
from jax.experimental import pallas as pl
from jax.experimental.pallas import tpu as pltpu
from jax.sharding import PartitionSpec as P

PARTS = 16
LINE = 4
COUNT = 4
ROWS = 16
LANES = 128
RING = 8
DEPTH = ROWS * LANES
GROUP = PARTS * COUNT
FAR_FIRST = (4, 3, 5, 2, 6, 1, 7, 0)


def dot(a, b):
    return lax.dot_general(a, b, (((1,), (0,)), ((), ())), preferred_element_type=jnp.float32)


def dot_nt(a, b):
    return lax.dot_general(a, b, (((1,), (1,)), ((), ())), preferred_element_type=jnp.float32)


def pick_lanes(value, pick):
    high = value.astype(jnp.bfloat16)
    rest = value - high.astype(jnp.float32)
    mid = rest.astype(jnp.bfloat16)
    low = (rest - mid.astype(jnp.float32)).astype(jnp.bfloat16)
    return dot(high, pick) + dot(mid, pick) + dot(low, pick)


def kernel(a_hbm, x_hbm, z_hbm, out_ref, mats, primal_ref, dual_ref, send1, recv1, send1_diag, recv1_diag, wide_rows,
           diag_rows, v_all, a_all, v_diag, a_diag, partial, halves, sibling, send3, recv3, joined,
           load, s1, r1, s1d, r1d, s2v, r2v, s2a, r2a, s2vd, r2vd, s2ad, r2ad, sh, rh, s3, r3, own_sem):
    wide, narrow = lax.axis_index("wide"), lax.axis_index("narrow")
    y = lax.rem(wide, 4)
    x = lax.rem(lax.div(wide, 4), 4)
    z_lo = lax.div(wide, 16)
    core = lax.rem(narrow, 2)
    z = lax.div(narrow, 2) * 4 + z_lo
    part = narrow * 4 + z_lo

    def device(x_at, y_at, z_at, core_at):
        return {"wide": lax.rem(z_at, 4) * 16 + x_at * 4 + y_at, "narrow": lax.div(z_at, 4) * 2 + core_at}

    def part_of(z_at, core_at):
        return (lax.div(z_at, 4) * 2 + core_at) * 4 + lax.rem(z_at, 4)

    column = [(lax.rem(z + dz, RING), lax.rem(core + dc, 2)) for dz in FAR_FIRST for dc in (0, 1) if dz or dc]
    owners = [(lax.rem(z + dz, RING), lax.rem(y + dy, LINE)) for dz in FAR_FIRST for dy in (2, 1, 3, 0) if dz or dy]
    line_x = [lax.rem(x + k, LINE) for k in (2, 1, 3)]
    line_y = [lax.rem(y + k, LINE) for k in (2, 1, 3)]

    loads = [pltpu.make_async_copy(x_hbm, primal_ref, load.at[4]), pltpu.make_async_copy(z_hbm, dual_ref, load.at[5])]
    for c in range(COUNT):
        loads.append(pltpu.make_async_copy(a_hbm.at[c], mats.at[c], load.at[c]))
    for copy in loads:
        copy.start()

    barrier = pltpu.get_barrier_semaphore()
    greeted = [device(x, y, z_at, core_at) for z_at, core_at in column]
    greeted += [device(x, y_at, lax.rem(z + dz, RING), core) for dz in FAR_FIRST[:-1] for y_at in line_y]
    greeted += [device(k, y, z, core) for k in line_x] + [device(x, k, z, core) for k in line_y]
    for peer in greeted:
        pl.semaphore_signal(barrier, inc=1, device_id=peer)

    def copy1(c, slot, z_to, core_to):
        to = part_of(z_to, core_to)
        return pltpu.make_async_remote_copy(
            src_ref=send1.at[c, to], dst_ref=recv1.at[c, slot], send_sem=s1.at[c, to], recv_sem=r1.at[c, slot],
            device_id=device(x, y, z_to, core_to),
        )

    def copy1_diag(slot, z_to, core_to):
        to = part_of(z_to, core_to)
        return pltpu.make_async_remote_copy(
            src_ref=send1_diag, dst_ref=recv1_diag.at[slot], send_sem=s1d.at[to], recv_sem=r1d.at[slot],
            device_id=device(x, y, z_to, core_to),
        )

    def own1(c):
        return pltpu.make_async_copy(send1.at[c, part], recv1.at[c, part], own_sem.at[c])

    row = lax.broadcasted_iota(jnp.int32, (LANES, LANES), 0)
    col = lax.broadcasted_iota(jnp.int32, (LANES, LANES), 1)
    loads[0].wait()
    loads[1].wait()
    primal, dual = primal_ref[...], dual_ref[...]
    diag_a, diag_v = [], []
    for c in range(COUNT):
        loads[2 + c].wait()
        mat = mats[c]
        left = dot(primal, mat).astype(jnp.bfloat16)
        top = dot(left[:LANES], dual) + dot_nt(dual[:LANES], left)
        low = dot(left[LANES:], dual[:, LANES:]) + dot_nt(dual[LANES:], left[LANES:])
        mat32 = mat.astype(jnp.float32)
        a_up, a_low = mat32[:LANES, :LANES], mat32[LANES:, LANES:]
        fold_a = [mat[:LANES, LANES:], jnp.where(row <= col, a_up, a_low).astype(jnp.bfloat16)]
        corner = jnp.where(row < col, top[:, :LANES], jnp.where(row == col, 0.5 * top[:, :LANES], low))
        fold_v = [top[:, LANES:].astype(jnp.bfloat16), corner.astype(jnp.bfloat16)]
        diag_a.append(jnp.sum(jnp.where(row == col, a_low, 0.0), axis=0, keepdims=True))
        diag_v.append(jnp.sum(jnp.where(row == col, low, 0.0), axis=0, keepdims=True) * (0.5 / PARTS))
        for d in range(PARTS):
            half, at = d // 8, (d % 8) * ROWS
            send1[c, d, :ROWS, :] = fold_a[half][at:at + ROWS]
            send1[c, d, ROWS:, :] = fold_v[half][at:at + ROWS]
        if c == COUNT - 1:
            send1_diag[...] = jnp.concatenate(diag_a + diag_v, axis=0).astype(jnp.bfloat16)
        if c == 0:
            pl.semaphore_wait(barrier, len(greeted))
        for z_to, core_to in column:
            copy1(c, part, z_to, core_to).start()
            if c == COUNT - 1:
                copy1_diag(part, z_to, core_to).start()
        own1(c).start()
    recv1_diag[part] = send1_diag[...]

    def copy2(ref, slot, c, sems, to):
        along, to = to
        peer = device(x, to, z, core) if along == "y" else device(to, y, z, core)
        at = ref.at[slot, c] if c is not None else ref.at[slot]
        where = (lambda k: (k, c)) if c is not None else (lambda k: (k,))
        return pltpu.make_async_remote_copy(
            src_ref=at, dst_ref=at, send_sem=sems[0].at[where(to)], recv_sem=sems[1].at[where(slot)], device_id=peer
        )

    def lines(c, sending):
        v, a, sv, sa = (v_all, a_all, (s2v, r2v), (s2a, r2a)) if c is not None else (v_diag, a_diag, (s2vd, r2vd), (s2ad, r2ad))
        copies = []
        for ky, kx in zip(line_y, line_x):
            copies.append(copy2(v, y if sending else ky, c, sv, ("y", ky)))
            copies.append(copy2(a, x if sending else kx, c, sa, ("x", kx)))
        return copies

    for c in range(COUNT):
        own1(c).wait()
        for z_from, core_from in reversed(column):
            copy1(c, part_of(z_from, core_from), z_from, core_from).wait_recv()
        for s in range(PARTS):
            block = recv1[c, s].astype(jnp.float32)
            wide_rows[c, 0, ROWS * s:ROWS * (s + 1), :] = block[:ROWS]
            wide_rows[c, 1, ROWS * s:ROWS * (s + 1), :] = block[ROWS:]
        for r in range(ROWS):
            at = pl.ds(r * LANES, LANES)
            a_all[x, c, :, at] = wide_rows[c, 0, pl.ds(r, PARTS, stride=ROWS), :].astype(jnp.bfloat16)
            v_all[y, c, :, at] = wide_rows[c, 1, pl.ds(r, PARTS, stride=ROWS), :].astype(jnp.bfloat16)
        for copy in lines(c, True):
            copy.start()
    for z_from, core_from in reversed(column):
        copy1_diag(part_of(z_from, core_from), z_from, core_from).wait_recv()
    for s in range(PARTS):
        diag_rows[pl.ds(RING * s, RING), :] = recv1_diag[s].astype(jnp.float32)
    for c in range(COUNT):
        at = slice(PARTS * c, PARTS * (c + 1))
        a_diag[x, at, :] = diag_rows[pl.ds(c, PARTS, stride=RING), :].astype(jnp.bfloat16)
        v_diag[y, at, :] = diag_rows[pl.ds(COUNT + c, PARTS, stride=RING), :].astype(jnp.bfloat16)
    for copy in lines(None, True):
        copy.start()
    for c in (*range(COUNT), None):
        for copy in lines(c, False):
            copy.wait_recv()

    size = LINE * GROUP
    product = dot_nt(v_all[...].reshape(size, DEPTH), a_all[...].reshape(size, DEPTH)) + dot_nt(
        v_diag[...].reshape(size, LANES), a_diag[...].reshape(size, LANES)
    )
    for h in range(2):
        partial[h] = product[:, LANES * h:LANES * (h + 1)]

    for core_to in range(2):
        for z_to in range(RING):
            p = (z_to // 4 * 2 + core_to) * 4 + z_to % 4
            for h in range(2):
                halves[core_to, z_to, :, LANES * h:LANES * (h + 1)] = partial[h, pl.ds(p, LINE * COUNT, stride=PARTS), :]
    other = lax.rem(core + 1, 2)
    swap = pltpu.make_async_remote_copy(
        src_ref=halves.at[other], dst_ref=sibling, send_sem=sh, recv_sem=rh, device_id=device(x, y, z, other)
    )
    swap.start()
    swap.wait_recv()
    for z_to in range(RING):
        both = halves[core, z_to] + sibling[z_to]
        for k in range(LINE):
            send3[z_to, k] = both[COUNT * k:COUNT * (k + 1)]

    def copy3(z_slot, y_slot, z_to, y_to):
        return pltpu.make_async_remote_copy(
            src_ref=send3.at[z_to, y_to], dst_ref=recv3.at[z_slot, y_slot], send_sem=s3.at[z_to, y_to],
            recv_sem=r3.at[z_slot, y_slot], device_id=device(x, y_to, z_to, core),
        )

    for z_to, y_to in owners:
        copy3(z, y, z_to, y_to).start()
    recv3[z, y] = send3[z, y]

    lane_from = lax.broadcasted_iota(jnp.int32, (size, size), 0)
    lane_to = lax.broadcasted_iota(jnp.int32, (size, size), 1)
    digit = lambda place: lax.rem(lax.div(lane_to, place), 4)
    first = digit(16) * 64 + digit(1) * 16 + digit(64) * 4 + digit(4)
    second = digit(4) * 64 + digit(16) * 16 + digit(64) * 4 + digit(1)
    pick1 = jnp.where(lane_from == first, 1.0, 0.0).astype(jnp.bfloat16)
    pick2 = jnp.where(lane_from == second, 1.0, 0.0).astype(jnp.bfloat16)

    for z_from, y_from in reversed(owners):
        copy3(z_from, y_from, z_from, y_from).wait_recv()
    rows = []
    for k in range(LINE):
        total = recv3[0, k]
        for z_from in range(1, RING):
            total = total + recv3[z_from, k]
        rows.append(total)
    grouped = pick_lanes(jnp.concatenate(rows, axis=0), pick1)
    for k in range(LINE):
        for n in range(LINE):
            joined[COUNT * n:COUNT * (n + 1), GROUP * k:GROUP * (k + 1)] = grouped[
                COUNT * k:COUNT * (k + 1), GROUP * n:GROUP * (n + 1)
            ]
    ordered = pick_lanes(joined[...], pick2)
    for n in range(LINE):
        out_ref[:, size * n:size * (n + 1)] = ordered[COUNT * n:COUNT * (n + 1)]

    for c in range(COUNT):
        for z_to, core_to in column:
            copy1(c, part, z_to, core_to).wait_send()
    for z_to, core_to in column:
        copy1_diag(part, z_to, core_to).wait_send()
    for c in (*range(COUNT), None):
        for copy in lines(c, True):
            copy.wait_send()
    swap.wait_send()
    for z_to, y_to in owners:
        copy3(z, y, z_to, y_to).wait_send()


def body(constraint_mats, primal_matrix, inverse_dual_iterate):
    hbm = pl.BlockSpec(memory_space=pltpu.HBM)
    dma = pltpu.SemaphoreType.DMA
    bf16, f32 = jnp.bfloat16, jnp.float32
    order = 2 * LANES
    size = LINE * GROUP
    return pl.pallas_call(
        kernel,
        out_shape=jax.ShapeDtypeStruct((COUNT, 1024), f32),
        in_specs=[hbm] * 3,
        out_specs=pl.BlockSpec(memory_space=pltpu.VMEM),
        scratch_shapes=[
            pltpu.VMEM((COUNT, order, order), bf16),
            pltpu.VMEM((order, order), bf16),
            pltpu.VMEM((order, order), bf16),
            pltpu.VMEM((COUNT, PARTS, 2 * ROWS, LANES), bf16),
            pltpu.VMEM((COUNT, PARTS, 2 * ROWS, LANES), bf16),
            pltpu.VMEM((2 * COUNT, LANES), bf16),
            pltpu.VMEM((PARTS, 2 * COUNT, LANES), bf16),
            pltpu.VMEM((COUNT, 2, PARTS * ROWS, LANES), f32),
            pltpu.VMEM((PARTS * 2 * COUNT, LANES), f32),
            pltpu.VMEM((LINE, COUNT, PARTS, DEPTH), bf16),
            pltpu.VMEM((LINE, COUNT, PARTS, DEPTH), bf16),
            pltpu.VMEM((LINE, GROUP, LANES), bf16),
            pltpu.VMEM((LINE, GROUP, LANES), bf16),
            pltpu.VMEM((2, size, LANES), f32),
            pltpu.VMEM((2, RING, LINE * COUNT, size), f32),
            pltpu.VMEM((RING, LINE * COUNT, size), f32),
            pltpu.VMEM((RING, LINE, COUNT, size), f32),
            pltpu.VMEM((RING, LINE, COUNT, size), f32),
            pltpu.VMEM((LINE * COUNT, size), f32),
            dma((6,)),
            dma((COUNT, PARTS)), dma((COUNT, PARTS)), dma((PARTS,)), dma((PARTS,)),
            dma((LINE, COUNT)), dma((LINE, COUNT)), dma((LINE, COUNT)), dma((LINE, COUNT)),
            dma((LINE,)), dma((LINE,)), dma((LINE,)), dma((LINE,)),
            dma, dma,
            dma((RING, LINE)), dma((RING, LINE)),
            dma((COUNT,)),
        ],
        compiler_params=pltpu.CompilerParams(collective_id=0, has_side_effects=True),
        name="schur",
    )(constraint_mats, primal_matrix, inverse_dual_iterate)


def solution(mesh):
    in_specs = (P(("narrow", "wide"), None, None), P(), P())
    out_specs = P(("narrow", "wide"), None)
    return jax.shard_map(body, mesh=mesh, in_specs=in_specs, out_specs=out_specs, check_vma=False)
```

time: 845 us -> 46.4 us (0.05)
  the two profiles are of different devices: /device:TPU:8 before, /device:TPU:1 now
where the time goes in v2:
time: 46.4 us; the launch traced here: 46.3 us
  Pallas kernels  44.9 us (97%)
  local copies, waits for them, and re-layouts  1.32 us (3%)
    pallas_call x1, Pallas kernels, body(): pl.pallas_call(kernel, out_shape=jax.ShapeDtypeStruct((COUNT, 1024), f32)...  44.9 us
    unnamed x1, local copies, waits for them, and re-layouts  1.32 us

profile of v2, /device:TPU:1, one launch (start us, length us, event | category | flops | bytes accessed | tf_op | source)
XLA Modules:
  0.0 46.3 jit_solution(11520079428487155587)
XLA Ops:
  0.0 44.9 %schur.1 = f32[4,1024]{1,0:T(4,128)} custom-call(bf16[4,256,256]{2,1,0:T(8,128)(2,1)} %a_hbm.1, bf16[256,256]{1,0:T(8,128)(2,1)} %x_hbm.1, bf16[256,256]{1,0:T(8,128)(2,1)} %z_hbm.1), custom_call_target="tpu_custom_call" | custom-call | tf_op jit(solution)/shard_map/schur/pallas_call | solution.py:244
  44.9 1.3 %copy.5 = f32[4,1024]{1,0:T(4,128)} copy(f32[4,1024]{1,0:T(4,128)} %schur.1) | data formatting | bytes 32768

commit v3 on v2

v3 whole, which is shorter than its diff:
```python
import jax
import jax.numpy as jnp
from jax import lax
from jax.experimental import pallas as pl
from jax.experimental.pallas import tpu as pltpu
from jax.sharding import PartitionSpec as P

PARTS = 16
LINE = 4
COUNT = 4
ROWS = 16
LANES = 128
RING = 8
DEPTH = ROWS * LANES
GROUP = PARTS * COUNT
FAR_FIRST = (4, 3, 5, 2, 6, 1, 7, 0)


def dot(a, b):
    return lax.dot_general(a, b, (((1,), (0,)), ((), ())), preferred_element_type=jnp.float32)


def dot_nt(a, b):
    return lax.dot_general(a, b, (((1,), (1,)), ((), ())), preferred_element_type=jnp.float32)


def pick_lanes(value, pick):
    high = value.astype(jnp.bfloat16)
    rest = value - high.astype(jnp.float32)
    mid = rest.astype(jnp.bfloat16)
    low = (rest - mid.astype(jnp.float32)).astype(jnp.bfloat16)
    return dot(high, pick) + dot(mid, pick) + dot(low, pick)


def kernel(a_hbm, x_hbm, z_hbm, out_ref, mats, primal_ref, dual_ref, send1, recv1, send1_diag, recv1_diag, wide_rows,
           diag_rows, v_all, a_all, v_diag, a_diag, partial, halves, sibling, send3, recv3, joined,
           load, s1, r1, s1d, r1d, s2, r2, s2d, r2d, sh, rh, s3, r3, own_sem):
    loads = [pltpu.make_async_copy(x_hbm, primal_ref, load.at[4]), pltpu.make_async_copy(z_hbm, dual_ref, load.at[5])]
    for c in range(COUNT):
        loads.append(pltpu.make_async_copy(a_hbm.at[c], mats.at[c], load.at[c]))
    for copy in loads:
        copy.start()

    wide, narrow = lax.axis_index("wide"), lax.axis_index("narrow")
    z_hi = lax.div(narrow, 2)
    core = narrow - 2 * z_hi
    z_lo = lax.div(wide, 16)
    plane = wide - 16 * z_lo
    x = lax.div(plane, 4)
    y = plane - 4 * x
    z = z_hi * 4 + z_lo
    part = narrow * 4 + z_lo

    def wrap(value, size):
        return jnp.where(value >= size, value - size, value)

    column, same_core = [], []
    for dz in FAR_FIRST:
        z_at = wrap(z + dz, RING)
        hi = jnp.where(z_at >= 4, 1, 0)
        lo = z_at - 4 * hi
        for other in (0, 1):
            narrow_at = 2 * hi + (1 - core if other else core)
            if dz or other:
                column.append((narrow_at * 4 + lo, {"wide": lo * 16 + plane, "narrow": narrow_at}))
        same_core.append((z_at, lo * 16 + x * 4, 2 * hi + core))
    line_x, line_y = [], []
    for k in (2, 1, 3):
        x_at, y_at = wrap(x + k, LINE), wrap(y + k, LINE)
        line_x.append((x_at, {"wide": z_lo * 16 + x_at * 4 + y, "narrow": narrow}))
        line_y.append((y_at, {"wide": wide - y + y_at, "narrow": narrow}))
    owners = [
        (z_at * LINE + y_at, {"wide": base + y_at, "narrow": narrow_at})
        for z_at, base, narrow_at in same_core[:-1] for y_at in [k for k, _ in line_y] + [y]
    ] + [(z * LINE + y_at, peer) for y_at, peer in line_y]
    sibling_core = {"wide": wide, "narrow": 2 * z_hi + 1 - core}

    barrier = pltpu.get_barrier_semaphore()
    greeted = [peer for _, peer in column + line_x + line_y]
    for peer in greeted:
        pl.semaphore_signal(barrier, inc=1, device_id=peer)

    def remote(src, dst, send_sem, recv_sem, peer):
        return pltpu.make_async_remote_copy(
            src_ref=src, dst_ref=dst, send_sem=send_sem, recv_sem=recv_sem, device_id=peer
        )

    def wait_bytes(like, sem):
        pltpu.make_async_copy(like, like, sem).wait()

    def own1(c):
        return pltpu.make_async_copy(send1.at[c, part], recv1.at[c, part], own_sem.at[c])

    row = lax.broadcasted_iota(jnp.int32, (LANES, LANES), 0)
    col = lax.broadcasted_iota(jnp.int32, (LANES, LANES), 1)
    loads[0].wait()
    loads[1].wait()
    primal, dual = primal_ref[...], dual_ref[...]
    diag_a, diag_v = [], []
    for c in range(COUNT):
        loads[2 + c].wait()
        mat = mats[c]
        left = dot(primal, mat).astype(jnp.bfloat16)
        top = dot(left[:LANES], dual) + dot_nt(dual[:LANES], left)
        low = dot(left[LANES:], dual[:, LANES:]) + dot_nt(dual[LANES:], left[LANES:])
        mat32 = mat.astype(jnp.float32)
        a_up, a_low = mat32[:LANES, :LANES], mat32[LANES:, LANES:]
        fold_a = [mat[:LANES, LANES:], jnp.where(row <= col, a_up, a_low).astype(jnp.bfloat16)]
        corner = jnp.where(row < col, top[:, :LANES], jnp.where(row == col, 0.5 * top[:, :LANES], low))
        fold_v = [top[:, LANES:].astype(jnp.bfloat16), corner.astype(jnp.bfloat16)]
        diag_a.append(jnp.sum(jnp.where(row == col, a_low, 0.0), axis=0, keepdims=True))
        diag_v.append(jnp.sum(jnp.where(row == col, low, 0.0), axis=0, keepdims=True) * (0.5 / PARTS))
        for d in range(PARTS):
            half, at = d // 8, (d % 8) * ROWS
            send1[c, d, :ROWS, :] = fold_a[half][at:at + ROWS]
            send1[c, d, ROWS:, :] = fold_v[half][at:at + ROWS]
        if c == 0:
            pl.semaphore_wait(barrier, len(greeted))
        if c == COUNT - 1:
            send1_diag[...] = jnp.concatenate(diag_a + diag_v, axis=0).astype(jnp.bfloat16)
            for _, peer in column:
                remote(send1_diag, recv1_diag.at[part], s1d, r1d, peer).start()
        for to, peer in column:
            remote(send1.at[c, to], recv1.at[c, part], s1.at[c], r1.at[c], peer).start()
        own1(c).start()
    recv1_diag[part] = send1_diag[...]

    def send_lines(v, a, send_sem, recv_sem):
        for (_, peer_y), (_, peer_x) in zip(line_y, line_x):
            remote(v(y), v(y), send_sem.at[0], recv_sem.at[0], peer_y).start()
            remote(a(x), a(x), send_sem.at[1], recv_sem.at[1], peer_x).start()

    for c in range(COUNT):
        if c == COUNT - 1:
            wait_bytes(recv1_diag.at[:PARTS - 1], r1d)
            for s in range(PARTS):
                diag_rows[pl.ds(RING * s, RING), :] = recv1_diag[s].astype(jnp.float32)
            for k in range(COUNT):
                at = slice(PARTS * k, PARTS * (k + 1))
                a_diag[x, at, :] = diag_rows[pl.ds(k, PARTS, stride=RING), :].astype(jnp.bfloat16)
                v_diag[y, at, :] = diag_rows[pl.ds(COUNT + k, PARTS, stride=RING), :].astype(jnp.bfloat16)
            send_lines(lambda k: v_diag.at[k], lambda k: a_diag.at[k], s2d, r2d)
        own1(c).wait()
        wait_bytes(recv1.at[c, :PARTS - 1], r1.at[c])
        for s in range(PARTS):
            block = recv1[c, s].astype(jnp.float32)
            wide_rows[c, 0, ROWS * s:ROWS * (s + 1), :] = block[:ROWS]
            wide_rows[c, 1, ROWS * s:ROWS * (s + 1), :] = block[ROWS:]
        for r in range(ROWS):
            at = pl.ds(r * LANES, LANES)
            a_all[x, c, :, at] = wide_rows[c, 0, pl.ds(r, PARTS, stride=ROWS), :].astype(jnp.bfloat16)
            v_all[y, c, :, at] = wide_rows[c, 1, pl.ds(r, PARTS, stride=ROWS), :].astype(jnp.bfloat16)
        send_lines(lambda k: v_all.at[k, c], lambda k: a_all.at[k, c], s2, r2)
    for k, (v, a) in enumerate(((v_all, v_diag), (a_all, a_diag))):
        wait_bytes(a.at[:LINE - 1], r2d.at[k])
        wait_bytes(v.at[:LINE - 1], r2.at[k])

    size = LINE * GROUP
    v_mat, v_end = v_all[...].reshape(size, DEPTH), v_diag[...].reshape(size, LANES)
    swaps = []
    for h in range(2):
        a_mat = a_all[2 * h:2 * h + 2].reshape(LANES, DEPTH)
        a_end = a_diag[2 * h:2 * h + 2].reshape(LANES, LANES)
        partial[h] = dot_nt(v_mat, a_mat) + dot_nt(v_end, a_end)
        for core_to in range(2):
            for z_to in range(RING):
                p = (z_to // 4 * 2 + core_to) * 4 + z_to % 4
                halves[core_to, h, z_to] = partial[h, pl.ds(p, LINE * COUNT, stride=PARTS), :]
        swaps.append(remote(halves.at[1 - core, h], sibling.at[h], sh.at[h], rh.at[h], sibling_core))
        swaps[h].start()
    for h in range(2):
        swaps[h].wait_recv()
        for z_to in range(RING):
            both = halves[core, h, z_to] + sibling[h, z_to]
            for k in range(LINE):
                send3[z_to * LINE + k, :, LANES * h:LANES * (h + 1)] = both[COUNT * k:COUNT * (k + 1)]
    own = z * LINE + y
    for to, peer in owners:
        remote(send3.at[to], recv3.at[own], s3, r3, peer).start()
    recv3[own] = send3[own]

    lane_from = lax.broadcasted_iota(jnp.int32, (size, size), 0)
    lane_to = lax.broadcasted_iota(jnp.int32, (size, size), 1)
    digit = lambda place: lax.rem(lax.div(lane_to, place), 4)
    first = digit(16) * 64 + digit(1) * 16 + digit(64) * 4 + digit(4)
    second = digit(4) * 64 + digit(16) * 16 + digit(64) * 4 + digit(1)
    pick1 = jnp.where(lane_from == first, 1.0, 0.0).astype(jnp.bfloat16)
    pick2 = jnp.where(lane_from == second, 1.0, 0.0).astype(jnp.bfloat16)

    wait_bytes(recv3.at[:RING * LINE - 1], r3)
    rows = []
    for k in range(LINE):
        total = recv3[k]
        for z_from in range(1, RING):
            total = total + recv3[z_from * LINE + k]
        rows.append(total)
    grouped = pick_lanes(jnp.concatenate(rows, axis=0), pick1)
    for k in range(LINE):
        for n in range(LINE):
            joined[COUNT * n:COUNT * (n + 1), GROUP * k:GROUP * (k + 1)] = grouped[
                COUNT * k:COUNT * (k + 1), GROUP * n:GROUP * (n + 1)
            ]
    ordered = pick_lanes(joined[...], pick2)
    for n in range(LINE):
        out_ref[:, size * n:size * (n + 1)] = ordered[COUNT * n:COUNT * (n + 1)]

    for c in range(COUNT):
        wait_bytes(recv1.at[c, :PARTS - 1], s1.at[c])
    wait_bytes(recv1_diag.at[:PARTS - 1], s1d)
    for k in range(2):
        wait_bytes(v_all.at[:LINE - 1], s2.at[k])
        wait_bytes(v_diag.at[:LINE - 1], s2d.at[k])
        swaps[k].wait_send()
    wait_bytes(recv3.at[:RING * LINE - 1], s3)


def body(constraint_mats, primal_matrix, inverse_dual_iterate):
    hbm = pl.BlockSpec(memory_space=pltpu.HBM)
    dma = pltpu.SemaphoreType.DMA
    bf16, f32 = jnp.bfloat16, jnp.float32
    order = 2 * LANES
    size = LINE * GROUP
    return pl.pallas_call(
        kernel,
        out_shape=jax.ShapeDtypeStruct((COUNT, 1024), f32),
        in_specs=[hbm] * 3,
        out_specs=pl.BlockSpec(memory_space=pltpu.VMEM),
        scratch_shapes=[
            pltpu.VMEM((COUNT, order, order), bf16),
            pltpu.VMEM((order, order), bf16),
            pltpu.VMEM((order, order), bf16),
            pltpu.VMEM((COUNT, PARTS, 2 * ROWS, LANES), bf16),
            pltpu.VMEM((COUNT, PARTS, 2 * ROWS, LANES), bf16),
            pltpu.VMEM((2 * COUNT, LANES), bf16),
            pltpu.VMEM((PARTS, 2 * COUNT, LANES), bf16),
            pltpu.VMEM((COUNT, 2, PARTS * ROWS, LANES), f32),
            pltpu.VMEM((PARTS * 2 * COUNT, LANES), f32),
            pltpu.VMEM((LINE, COUNT, PARTS, DEPTH), bf16),
            pltpu.VMEM((LINE, COUNT, PARTS, DEPTH), bf16),
            pltpu.VMEM((LINE, GROUP, LANES), bf16),
            pltpu.VMEM((LINE, GROUP, LANES), bf16),
            pltpu.VMEM((2, size, LANES), f32),
            pltpu.VMEM((2, 2, RING, LINE * COUNT, LANES), f32),
            pltpu.VMEM((2, RING, LINE * COUNT, LANES), f32),
            pltpu.VMEM((RING * LINE, COUNT, size), f32),
            pltpu.VMEM((RING * LINE, COUNT, size), f32),
            pltpu.VMEM((LINE * COUNT, size), f32),
            dma((6,)),
            dma((COUNT,)), dma((COUNT,)), dma, dma,
            dma((2,)), dma((2,)), dma((2,)), dma((2,)),
            dma((2,)), dma((2,)), dma, dma,
            dma((COUNT,)),
        ],
        compiler_params=pltpu.CompilerParams(collective_id=0, has_side_effects=True),
        name="schur",
    )(constraint_mats, primal_matrix, inverse_dual_iterate)


def solution(mesh):
    in_specs = (P(("narrow", "wide"), None, None), P(), P())
    out_specs = P(("narrow", "wide"), None)
    return jax.shard_map(body, mesh=mesh, in_specs=in_specs, out_specs=out_specs, check_vma=False)
```

time: 46.4 us -> 43.6 us (0.940)
  Pallas kernels: 44.9 us -> 42.1 us
    pallas_call x1, Pallas kernels: 44.9 us -> 42.1 us  [body(): pl.pallas_call(kernel, out_shape=jax.ShapeDtypeStruct((COUNT, 1024), f32)...]
where the time goes in v3:
time: 43.6 us; the launch traced here: 43.4 us
  Pallas kernels  42.1 us (97%)
  local copies, waits for them, and re-layouts  1.32 us (3%)
    pallas_call x1, Pallas kernels, body(): pl.pallas_call(kernel, out_shape=jax.ShapeDtypeStruct((COUNT, 1024), f32)...  42.1 us
    unnamed x1, local copies, waits for them, and re-layouts  1.32 us

profile of v3, /device:TPU:1, one launch (start us, length us, event | category | flops | bytes accessed | tf_op | source)
XLA Modules:
  0.0 43.4 jit_solution(6618698065858551740)
XLA Ops:
  0.0 42.1 %schur.1 = f32[4,1024]{1,0:T(4,128)} custom-call(bf16[4,256,256]{2,1,0:T(8,128)(2,1)} %a_hbm.1, bf16[256,256]{1,0:T(8,128)(2,1)} %x_hbm.1, bf16[256,256]{1,0:T(8,128)(2,1)} %z_hbm.1), custom_call_target="tpu_custom_call" | custom-call | tf_op jit(solution)/shard_map/schur/pallas_call | solution.py:223
  42.1 1.3 %copy.5 = f32[4,1024]{1,0:T(4,128)} copy(f32[4,1024]{1,0:T(4,128)} %schur.1) | data formatting | bytes 32768

commit v4 on v3

--- a/solution.py
+++ b/solution.py
@@ -34,7 +34,7 @@
 
 def kernel(a_hbm, x_hbm, z_hbm, out_ref, mats, primal_ref, dual_ref, send1, recv1, send1_diag, recv1_diag, wide_rows,
            diag_rows, v_all, a_all, v_diag, a_diag, partial, halves, sibling, send3, recv3, joined,
-           load, s1, r1, s1d, r1d, s2, r2, s2d, r2d, sh, rh, s3, r3, own_sem):
+           load, s1, r1, s1d, r1d, s2, r2, sf, rf, s2d, r2d, sh, rh, s3, r3, own_sem):
     loads = [pltpu.make_async_copy(x_hbm, primal_ref, load.at[4]), pltpu.make_async_copy(z_hbm, dual_ref, load.at[5])]
     for c in range(COUNT):
         loads.append(pltpu.make_async_copy(a_hbm.at[c], mats.at[c], load.at[c]))
@@ -125,10 +125,20 @@
         own1(c).start()
     recv1_diag[part] = send1_diag[...]
 
-    def send_lines(v, a, send_sem, recv_sem):
-        for (_, peer_y), (_, peer_x) in zip(line_y, line_x):
-            remote(v(y), v(y), send_sem.at[0], recv_sem.at[0], peer_y).start()
-            remote(a(x), a(x), send_sem.at[1], recv_sem.at[1], peer_x).start()
+    axes = ((v_all, v_diag, y, line_y), (a_all, a_diag, x, line_x))
+    lanes = (slice(0, DEPTH // 2), slice(DEPTH // 2, DEPTH))
+
+    def send_neighbours(c):
+        for k, (ref, _, me, line) in enumerate(axes):
+            for _, peer in line[1:]:
+                remote(ref.at[me, c], ref.at[me, c], s2.at[k], r2.at[c, k], peer).start()
+
+    def forward(c):
+        for k, (ref, _, _, line) in enumerate(axes):
+            wait_bytes(ref.at[:2, c], r2.at[c, k])
+            for (source, _), (_, peer), half in zip(line[1:], reversed(line[1:]), lanes):
+                at = ref.at[source, c, :, half]
+                remote(at, at, sf.at[k], rf.at[k], peer).start()
 
     for c in range(COUNT):
         if c == COUNT - 1:
@@ -139,7 +149,9 @@
                 at = slice(PARTS * k, PARTS * (k + 1))
                 a_diag[x, at, :] = diag_rows[pl.ds(k, PARTS, stride=RING), :].astype(jnp.bfloat16)
                 v_diag[y, at, :] = diag_rows[pl.ds(COUNT + k, PARTS, stride=RING), :].astype(jnp.bfloat16)
-            send_lines(lambda k: v_diag.at[k], lambda k: a_diag.at[k], s2d, r2d)
+            for k, (_, ref, me, line) in enumerate(axes):
+                for _, peer in line:
+                    remote(ref.at[me], ref.at[me], s2d.at[k], r2d.at[k], peer).start()
         own1(c).wait()
         wait_bytes(recv1.at[c, :PARTS - 1], r1.at[c])
         for s in range(PARTS):
@@ -150,18 +162,20 @@
             at = pl.ds(r * LANES, LANES)
             a_all[x, c, :, at] = wide_rows[c, 0, pl.ds(r, PARTS, stride=ROWS), :].astype(jnp.bfloat16)
             v_all[y, c, :, at] = wide_rows[c, 1, pl.ds(r, PARTS, stride=ROWS), :].astype(jnp.bfloat16)
-        send_lines(lambda k: v_all.at[k, c], lambda k: a_all.at[k, c], s2, r2)
-    for k, (v, a) in enumerate(((v_all, v_diag), (a_all, a_diag))):
-        wait_bytes(a.at[:LINE - 1], r2d.at[k])
-        wait_bytes(v.at[:LINE - 1], r2.at[k])
+        send_neighbours(c)
+        if c:
+            forward(c - 1)
+    forward(COUNT - 1)
+    for k, (ref, ref_diag, _, _) in enumerate(axes):
+        wait_bytes(ref_diag.at[:LINE - 1], r2d.at[k])
+        wait_bytes(ref.at[0], rf.at[k])
 
     size = LINE * GROUP
     v_mat, v_end = v_all[...].reshape(size, DEPTH), v_diag[...].reshape(size, LANES)
+    product = dot_nt(v_mat, a_all[...].reshape(size, DEPTH)) + dot_nt(v_end, a_diag[...].reshape(size, LANES))
     swaps = []
     for h in range(2):
-        a_mat = a_all[2 * h:2 * h + 2].reshape(LANES, DEPTH)
-        a_end = a_diag[2 * h:2 * h + 2].reshape(LANES, LANES)
-        partial[h] = dot_nt(v_mat, a_mat) + dot_nt(v_end, a_end)
+        partial[h] = product[:, LANES * h:LANES * (h + 1)]
         for core_to in range(2):
             for z_to in range(RING):
                 p = (z_to // 4 * 2 + core_to) * 4 + z_to % 4
@@ -208,7 +222,8 @@
         wait_bytes(recv1.at[c, :PARTS - 1], s1.at[c])
     wait_bytes(recv1_diag.at[:PARTS - 1], s1d)
     for k in range(2):
-        wait_bytes(v_all.at[:LINE - 1], s2.at[k])
+        wait_bytes(v_all.at[:2], s2.at[k])
+        wait_bytes(v_all.at[0], sf.at[k])
         wait_bytes(v_diag.at[:LINE - 1], s2d.at[k])
         swaps[k].wait_send()
     wait_bytes(recv3.at[:RING * LINE - 1], s3)
@@ -247,7 +262,7 @@
             pltpu.VMEM((LINE * COUNT, size), f32),
             dma((6,)),
             dma((COUNT,)), dma((COUNT,)), dma, dma,
-            dma((2,)), dma((2,)), dma((2,)), dma((2,)),
+            dma((2,)), dma((COUNT, 2)), dma((2,)), dma((2,)), dma((2,)), dma((2,)),
             dma((2,)), dma((2,)), dma, dma,
             dma((COUNT,)),
         ],

time: 43.6 us -> 43.8 us (level)
  no operation moved by 1% of the time
where the time goes in v4:
time: 43.8 us; the launch traced here: 43.6 us
  Pallas kernels  42.3 us (97%)
  local copies, waits for them, and re-layouts  1.32 us (3%)
    pallas_call x1, Pallas kernels, body(): pl.pallas_call(kernel, out_shape=jax.ShapeDtypeStruct((COUNT, 1024), f32)...  42.3 us
    unnamed x1, local copies, waits for them, and re-layouts  1.32 us

profile of v4, /device:TPU:1, one launch (start us, length us, event | category | flops | bytes accessed | tf_op | source)
XLA Modules:
  0.0 43.6 jit_solution(8521995914192777892)
XLA Ops:
  0.0 42.3 %schur.1 = f32[4,1024]{1,0:T(4,128)} custom-call(bf16[4,256,256]{2,1,0:T(8,128)(2,1)} %a_hbm.1, bf16[256,256]{1,0:T(8,128)(2,1)} %x_hbm.1, bf16[256,256]{1,0:T(8,128)(2,1)} %z_hbm.1), custom_call_target="tpu_custom_call" | custom-call | tf_op jit(solution)/shard_map/schur/pallas_call | solution.py:238
  42.3 1.3 %copy.5 = f32[4,1024]{1,0:T(4,128)} copy(f32[4,1024]{1,0:T(4,128)} %schur.1) | data formatting | bytes 32768

commit v5 on v3

--- a/solution.py
+++ b/solution.py
@@ -14,6 +14,8 @@
 DEPTH = ROWS * LANES
 GROUP = PARTS * COUNT
 FAR_FIRST = (4, 3, 5, 2, 6, 1, 7, 0)
+CHUNKS = ((0, 0, 16), (1, 0, 16), (2, 0, 16), (3, 0, 8), (3, 8, 16))
+FORWARDED = 3
 
 
 def dot(a, b):
@@ -34,7 +36,7 @@
 
 def kernel(a_hbm, x_hbm, z_hbm, out_ref, mats, primal_ref, dual_ref, send1, recv1, send1_diag, recv1_diag, wide_rows,
            diag_rows, v_all, a_all, v_diag, a_diag, partial, halves, sibling, send3, recv3, joined,
-           load, s1, r1, s1d, r1d, s2, r2, s2d, r2d, sh, rh, s3, r3, own_sem):
+           load, s1, r1, s1d, r1d, s2, r2, sf, rf, s2d, r2d, sh, rh, s3, r3, own_sem):
     loads = [pltpu.make_async_copy(x_hbm, primal_ref, load.at[4]), pltpu.make_async_copy(z_hbm, dual_ref, load.at[5])]
     for c in range(COUNT):
         loads.append(pltpu.make_async_copy(a_hbm.at[c], mats.at[c], load.at[c]))
@@ -69,10 +71,6 @@
         x_at, y_at = wrap(x + k, LINE), wrap(y + k, LINE)
         line_x.append((x_at, {"wide": z_lo * 16 + x_at * 4 + y, "narrow": narrow}))
         line_y.append((y_at, {"wide": wide - y + y_at, "narrow": narrow}))
-    owners = [
-        (z_at * LINE + y_at, {"wide": base + y_at, "narrow": narrow_at})
-        for z_at, base, narrow_at in same_core[:-1] for y_at in [k for k, _ in line_y] + [y]
-    ] + [(z * LINE + y_at, peer) for y_at, peer in line_y]
     sibling_core = {"wide": wide, "narrow": 2 * z_hi + 1 - core}
 
     barrier = pltpu.get_barrier_semaphore()
@@ -88,8 +86,13 @@
     def wait_bytes(like, sem):
         pltpu.make_async_copy(like, like, sem).wait()
 
-    def own1(c):
-        return pltpu.make_async_copy(send1.at[c, part], recv1.at[c, part], own_sem.at[c])
+    def rows_of(k):
+        c, start, stop = CHUNKS[k]
+        return c, slice(2 * start, 2 * stop)
+
+    def own1(k):
+        c, rows = rows_of(k)
+        return pltpu.make_async_copy(send1.at[c, part, rows], recv1.at[c, part, rows], own_sem.at[k])
 
     row = lax.broadcasted_iota(jnp.int32, (LANES, LANES), 0)
     col = lax.broadcasted_iota(jnp.int32, (LANES, LANES), 1)
@@ -112,71 +115,105 @@
         diag_v.append(jnp.sum(jnp.where(row == col, low, 0.0), axis=0, keepdims=True) * (0.5 / PARTS))
         for d in range(PARTS):
             half, at = d // 8, (d % 8) * ROWS
-            send1[c, d, :ROWS, :] = fold_a[half][at:at + ROWS]
-            send1[c, d, ROWS:, :] = fold_v[half][at:at + ROWS]
+            for _, start, stop in [chunk for chunk in CHUNKS if chunk[0] == c]:
+                send1[c, d, 2 * start:start + stop, :] = fold_a[half][at + start:at + stop]
+                send1[c, d, start + stop:2 * stop, :] = fold_v[half][at + start:at + stop]
         if c == 0:
             pl.semaphore_wait(barrier, len(greeted))
         if c == COUNT - 1:
             send1_diag[...] = jnp.concatenate(diag_a + diag_v, axis=0).astype(jnp.bfloat16)
             for _, peer in column:
                 remote(send1_diag, recv1_diag.at[part], s1d, r1d, peer).start()
-        for to, peer in column:
-            remote(send1.at[c, to], recv1.at[c, part], s1.at[c], r1.at[c], peer).start()
-        own1(c).start()
+        for k, chunk in enumerate(CHUNKS):
+            if chunk[0] == c:
+                _, rows = rows_of(k)
+                for to, peer in column:
+                    remote(send1.at[c, to, rows], recv1.at[c, part, rows], s1.at[k], r1.at[k], peer).start()
+                own1(k).start()
     recv1_diag[part] = send1_diag[...]
 
-    def send_lines(v, a, send_sem, recv_sem):
-        for (_, peer_y), (_, peer_x) in zip(line_y, line_x):
-            remote(v(y), v(y), send_sem.at[0], recv_sem.at[0], peer_y).start()
-            remote(a(x), a(x), send_sem.at[1], recv_sem.at[1], peer_x).start()
-
-    for c in range(COUNT):
-        if c == COUNT - 1:
+    axes = ((v_all, v_diag, y, line_y), (a_all, a_diag, x, line_x))
+
+    def lanes_of(k):
+        _, start, stop = CHUNKS[k]
+        return slice(start * LANES, stop * LANES)
+
+    def send_lines(k):
+        for axis, (ref, _, me, line) in enumerate(axes):
+            at = ref.at[me, CHUNKS[k][0], :, lanes_of(k)]
+            for _, peer in line[1 if k < FORWARDED else 0:]:
+                remote(at, at, s2.at[k, axis], r2.at[k, axis], peer).start()
+
+    def forward(k):
+        c = CHUNKS[k][0]
+        for axis, (ref, _, _, line) in enumerate(axes):
+            wait_bytes(ref.at[:2, c], r2.at[k, axis])
+            for half, (source, _), (_, peer) in zip(range(2), line[1:], reversed(line[1:])):
+                at = ref.at[source, c, :, half * (DEPTH // 2):(half + 1) * (DEPTH // 2)]
+                remote(at, at, sf.at[axis], rf.at[axis], peer).start()
+
+    for k, (c, start, stop) in enumerate(CHUNKS):
+        if k == FORWARDED:
             wait_bytes(recv1_diag.at[:PARTS - 1], r1d)
             for s in range(PARTS):
                 diag_rows[pl.ds(RING * s, RING), :] = recv1_diag[s].astype(jnp.float32)
-            for k in range(COUNT):
-                at = slice(PARTS * k, PARTS * (k + 1))
-                a_diag[x, at, :] = diag_rows[pl.ds(k, PARTS, stride=RING), :].astype(jnp.bfloat16)
-                v_diag[y, at, :] = diag_rows[pl.ds(COUNT + k, PARTS, stride=RING), :].astype(jnp.bfloat16)
-            send_lines(lambda k: v_diag.at[k], lambda k: a_diag.at[k], s2d, r2d)
-        own1(c).wait()
-        wait_bytes(recv1.at[c, :PARTS - 1], r1.at[c])
+            for i in range(COUNT):
+                at = slice(PARTS * i, PARTS * (i + 1))
+                a_diag[x, at, :] = diag_rows[pl.ds(i, PARTS, stride=RING), :].astype(jnp.bfloat16)
+                v_diag[y, at, :] = diag_rows[pl.ds(COUNT + i, PARTS, stride=RING), :].astype(jnp.bfloat16)
+            for axis, (_, ref, me, line) in enumerate(axes):
+                for _, peer in line:
+                    remote(ref.at[me], ref.at[me], s2d.at[axis], r2d.at[axis], peer).start()
+        size = stop - start
+        own1(k).wait()
+        wait_bytes(recv1.at[c, :PARTS - 1, rows_of(k)[1]], r1.at[k])
         for s in range(PARTS):
-            block = recv1[c, s].astype(jnp.float32)
-            wide_rows[c, 0, ROWS * s:ROWS * (s + 1), :] = block[:ROWS]
-            wide_rows[c, 1, ROWS * s:ROWS * (s + 1), :] = block[ROWS:]
-        for r in range(ROWS):
-            at = pl.ds(r * LANES, LANES)
-            a_all[x, c, :, at] = wide_rows[c, 0, pl.ds(r, PARTS, stride=ROWS), :].astype(jnp.bfloat16)
-            v_all[y, c, :, at] = wide_rows[c, 1, pl.ds(r, PARTS, stride=ROWS), :].astype(jnp.bfloat16)
-        send_lines(lambda k: v_all.at[k, c], lambda k: a_all.at[k, c], s2, r2)
-    for k, (v, a) in enumerate(((v_all, v_diag), (a_all, a_diag))):
-        wait_bytes(a.at[:LINE - 1], r2d.at[k])
-        wait_bytes(v.at[:LINE - 1], r2.at[k])
+            block = recv1[c, s, 2 * start:2 * stop, :].astype(jnp.float32)
+            wide_rows[k, 0, size * s:size * (s + 1), :] = block[:size]
+            wide_rows[k, 1, size * s:size * (s + 1), :] = block[size:]
+        for r in range(size):
+            at = pl.ds((start + r) * LANES, LANES)
+            a_all[x, c, :, at] = wide_rows[k, 0, pl.ds(r, PARTS, stride=size), :].astype(jnp.bfloat16)
+            v_all[y, c, :, at] = wide_rows[k, 1, pl.ds(r, PARTS, stride=size), :].astype(jnp.bfloat16)
+        send_lines(k)
+        if 0 < k <= FORWARDED:
+            forward(k - 1)
+    for axis, (ref, ref_diag, _, _) in enumerate(axes):
+        wait_bytes(ref_diag.at[:LINE - 1], r2d.at[axis])
+        wait_bytes(ref.at[0, :FORWARDED], rf.at[axis])
+        for k in range(FORWARDED, len(CHUNKS)):
+            wait_bytes(ref.at[:LINE - 1, CHUNKS[k][0], :, lanes_of(k)], r2.at[k, axis])
 
     size = LINE * GROUP
     v_mat, v_end = v_all[...].reshape(size, DEPTH), v_diag[...].reshape(size, LANES)
+    product = dot_nt(v_mat, a_all[...].reshape(size, DEPTH)) + dot_nt(v_end, a_diag[...].reshape(size, LANES))
+    for h in range(2):
+        partial[h] = product[:, LANES * h:LANES * (h + 1)]
+
+    def rows_for(owner, h):
+        return partial[h, pl.ds(owner, LINE * COUNT, stride=PARTS), :]
+
     swaps = []
-    for h in range(2):
-        a_mat = a_all[2 * h:2 * h + 2].reshape(LANES, DEPTH)
-        a_end = a_diag[2 * h:2 * h + 2].reshape(LANES, LANES)
-        partial[h] = dot_nt(v_mat, a_mat) + dot_nt(v_end, a_end)
-        for core_to in range(2):
-            for z_to in range(RING):
-                p = (z_to // 4 * 2 + core_to) * 4 + z_to % 4
-                halves[core_to, h, z_to] = partial[h, pl.ds(p, LINE * COUNT, stride=PARTS), :]
-        swaps.append(remote(halves.at[1 - core, h], sibling.at[h], sh.at[h], rh.at[h], sibling_core))
-        swaps[h].start()
-    for h in range(2):
-        swaps[h].wait_recv()
-        for z_to in range(RING):
-            both = halves[core, h, z_to] + sibling[h, z_to]
+    for i, (z_at, base, narrow_at) in enumerate(same_core):
+        lo = jnp.where(z_at >= 4, z_at - 4, z_at)
+        for h in range(2):
+            halves[i, h] = rows_for((narrow_at + 1 - 2 * core) * 4 + lo, h)
+        swaps.append(remote(halves.at[i], sibling.at[i], sh.at[i], rh.at[i], sibling_core))
+        swaps[i].start()
+    own = z * LINE + y
+    for i, (z_at, base, narrow_at) in enumerate(same_core):
+        lo = jnp.where(z_at >= 4, z_at - 4, z_at)
+        swaps[i].wait_recv()
+        for h in range(2):
+            both = rows_for(narrow_at * 4 + lo, h) + sibling[i, h]
             for k in range(LINE):
-                send3[z_to * LINE + k, :, LANES * h:LANES * (h + 1)] = both[COUNT * k:COUNT * (k + 1)]
-    own = z * LINE + y
-    for to, peer in owners:
-        remote(send3.at[to], recv3.at[own], s3, r3, peer).start()
+                send3[z_at * LINE + k, :, LANES * h:LANES * (h + 1)] = both[COUNT * k:COUNT * (k + 1)]
+        for y_at, _ in line_y:
+            peer = {"wide": base + y_at, "narrow": narrow_at}
+            remote(send3.at[z_at * LINE + y_at], recv3.at[own], s3, r3, peer).start()
+        if i < RING - 1:
+            peer = {"wide": base + y, "narrow": narrow_at}
+            remote(send3.at[z_at * LINE + y], recv3.at[own], s3, r3, peer).start()
     recv3[own] = send3[own]
 
     lane_from = lax.broadcasted_iota(jnp.int32, (size, size), 0)
@@ -204,13 +241,16 @@
     for n in range(LINE):
         out_ref[:, size * n:size * (n + 1)] = ordered[COUNT * n:COUNT * (n + 1)]
 
-    for c in range(COUNT):
-        wait_bytes(recv1.at[c, :PARTS - 1], s1.at[c])
+    for k, (c, _, _) in enumerate(CHUNKS):
+        wait_bytes(recv1.at[c, :PARTS - 1, rows_of(k)[1]], s1.at[k])
+        for axis in range(2):
+            wait_bytes(v_all.at[:2 if k < FORWARDED else LINE - 1, c, :, lanes_of(k)], s2.at[k, axis])
     wait_bytes(recv1_diag.at[:PARTS - 1], s1d)
-    for k in range(2):
-        wait_bytes(v_all.at[:LINE - 1], s2.at[k])
-        wait_bytes(v_diag.at[:LINE - 1], s2d.at[k])
-        swaps[k].wait_send()
+    for axis in range(2):
+        wait_bytes(v_all.at[0, :FORWARDED], sf.at[axis])
+        wait_bytes(v_diag.at[:LINE - 1], s2d.at[axis])
+    for swap in swaps:
+        swap.wait_send()
     wait_bytes(recv3.at[:RING * LINE - 1], s3)
 
 
@@ -233,23 +273,23 @@
             pltpu.VMEM((COUNT, PARTS, 2 * ROWS, LANES), bf16),
             pltpu.VMEM((2 * COUNT, LANES), bf16),
             pltpu.VMEM((PARTS, 2 * COUNT, LANES), bf16),
-            pltpu.VMEM((COUNT, 2, PARTS * ROWS, LANES), f32),
+            pltpu.VMEM((len(CHUNKS), 2, PARTS * ROWS, LANES), f32),
             pltpu.VMEM((PARTS * 2 * COUNT, LANES), f32),
             pltpu.VMEM((LINE, COUNT, PARTS, DEPTH), bf16),
             pltpu.VMEM((LINE, COUNT, PARTS, DEPTH), bf16),
             pltpu.VMEM((LINE, GROUP, LANES), bf16),
             pltpu.VMEM((LINE, GROUP, LANES), bf16),
             pltpu.VMEM((2, size, LANES), f32),
-            pltpu.VMEM((2, 2, RING, LINE * COUNT, LANES), f32),
-            pltpu.VMEM((2, RING, LINE * COUNT, LANES), f32),
+            pltpu.VMEM((RING, 2, LINE * COUNT, LANES), f32),
+            pltpu.VMEM((RING, 2, LINE * COUNT, LANES), f32),
             pltpu.VMEM((RING * LINE, COUNT, size), f32),
             pltpu.VMEM((RING * LINE, COUNT, size), f32),
             pltpu.VMEM((LINE * COUNT, size), f32),
-            dma((6,)),
-            dma((COUNT,)), dma((COUNT,)), dma, dma,
-            dma((2,)), dma((2,)), dma((2,)), dma((2,)),
-            dma((2,)), dma((2,)), dma, dma,
-            dma((COUNT,)),
+            dma((COUNT + 2,)),
+            dma((len(CHUNKS),)), dma((len(CHUNKS),)), dma, dma,
+            dma((len(CHUNKS), 2)), dma((len(CHUNKS), 2)), dma((2,)), dma((2,)), dma((2,)), dma((2,)),
+            dma((RING,)), dma((RING,)), dma, dma,
+            dma((len(CHUNKS),)),
         ],
         compiler_params=pltpu.CompilerParams(collective_id=0, has_side_effects=True),
         name="schur",

time: 43.6 us -> 42.9 us (0.984)
  Pallas kernels: 42.1 us -> 41.3 us
    pallas_call x1, Pallas kernels: 42.1 us -> 41.3 us  [body(): pl.pallas_call(kernel, out_shape=jax.ShapeDtypeStruct((COUNT, 1024), f32)...]
where the time goes in v5:
time: 42.9 us; the launch traced here: 42.7 us
  Pallas kernels  41.3 us (96%)
  local copies, waits for them, and re-layouts  1.32 us (3%)
    pallas_call x1, Pallas kernels, body(): pl.pallas_call(kernel, out_shape=jax.ShapeDtypeStruct((COUNT, 1024), f32)...  41.3 us
    unnamed x1, local copies, waits for them, and re-layouts  1.32 us

profile of v5, /device:TPU:1, one launch (start us, length us, event | category | flops | bytes accessed | tf_op | source)
XLA Modules:
  0.0 42.7 jit_solution(6580152417829702432)
XLA Ops:
  0.0 41.3 %schur.1 = f32[4,1024]{1,0:T(4,128)} custom-call(bf16[4,256,256]{2,1,0:T(8,128)(2,1)} %a_hbm.1, bf16[256,256]{1,0:T(8,128)(2,1)} %x_hbm.1, bf16[256,256]{1,0:T(8,128)(2,1)} %z_hbm.1), custom_call_target="tpu_custom_call" | custom-call | tf_op jit(solution)/shard_map/schur/pallas_call | solution.py:263
  41.4 1.3 %copy.5 = f32[4,1024]{1,0:T(4,128)} copy(f32[4,1024]{1,0:T(4,128)} %schur.1) | data formatting | bytes 32768

commit v6 on v5

--- a/solution.py
+++ b/solution.py
@@ -14,8 +14,8 @@
 DEPTH = ROWS * LANES
 GROUP = PARTS * COUNT
 FAR_FIRST = (4, 3, 5, 2, 6, 1, 7, 0)
-CHUNKS = ((0, 0, 16), (1, 0, 16), (2, 0, 16), (3, 0, 8), (3, 8, 16))
-FORWARDED = 3
+CHUNKS = tuple((c, start, start + 8) for c in range(COUNT) for start in (0, 8))
+DIAG_CHUNK = len(CHUNKS) - 2
 
 
 def dot(a, b):
@@ -36,13 +36,7 @@
 
 def kernel(a_hbm, x_hbm, z_hbm, out_ref, mats, primal_ref, dual_ref, send1, recv1, send1_diag, recv1_diag, wide_rows,
            diag_rows, v_all, a_all, v_diag, a_diag, partial, halves, sibling, send3, recv3, joined,
-           load, s1, r1, s1d, r1d, s2, r2, sf, rf, s2d, r2d, sh, rh, s3, r3, own_sem):
-    loads = [pltpu.make_async_copy(x_hbm, primal_ref, load.at[4]), pltpu.make_async_copy(z_hbm, dual_ref, load.at[5])]
-    for c in range(COUNT):
-        loads.append(pltpu.make_async_copy(a_hbm.at[c], mats.at[c], load.at[c]))
-    for copy in loads:
-        copy.start()
-
+           load, s1, r1, s1d, r1d, s2, r2, s2d, r2d, sh, rh, s3, r3, own_sem):
     wide, narrow = lax.axis_index("wide"), lax.axis_index("narrow")
     z_hi = lax.div(narrow, 2)
     core = narrow - 2 * z_hi
@@ -77,6 +71,12 @@
     greeted = [peer for _, peer in column + line_x + line_y]
     for peer in greeted:
         pl.semaphore_signal(barrier, inc=1, device_id=peer)
+
+    loads = [pltpu.make_async_copy(x_hbm, primal_ref, load.at[4]), pltpu.make_async_copy(z_hbm, dual_ref, load.at[5])]
+    for c in range(COUNT):
+        loads.append(pltpu.make_async_copy(a_hbm.at[c], mats.at[c], load.at[c]))
+    for copy in loads:
+        copy.start()
 
     def remote(src, dst, send_sem, recv_sem, peer):
         return pltpu.make_async_remote_copy(
@@ -141,19 +141,11 @@
     def send_lines(k):
         for axis, (ref, _, me, line) in enumerate(axes):
             at = ref.at[me, CHUNKS[k][0], :, lanes_of(k)]
-            for _, peer in line[1 if k < FORWARDED else 0:]:
-                remote(at, at, s2.at[k, axis], r2.at[k, axis], peer).start()
-
-    def forward(k):
-        c = CHUNKS[k][0]
-        for axis, (ref, _, _, line) in enumerate(axes):
-            wait_bytes(ref.at[:2, c], r2.at[k, axis])
-            for half, (source, _), (_, peer) in zip(range(2), line[1:], reversed(line[1:])):
-                at = ref.at[source, c, :, half * (DEPTH // 2):(half + 1) * (DEPTH // 2)]
-                remote(at, at, sf.at[axis], rf.at[axis], peer).start()
+            for _, peer in line:
+                remote(at, at, s2.at[axis], r2.at[axis], peer).start()
 
     for k, (c, start, stop) in enumerate(CHUNKS):
-        if k == FORWARDED:
+        if k == DIAG_CHUNK:
             wait_bytes(recv1_diag.at[:PARTS - 1], r1d)
             for s in range(PARTS):
                 diag_rows[pl.ds(RING * s, RING), :] = recv1_diag[s].astype(jnp.float32)
@@ -176,13 +168,9 @@
             a_all[x, c, :, at] = wide_rows[k, 0, pl.ds(r, PARTS, stride=size), :].astype(jnp.bfloat16)
             v_all[y, c, :, at] = wide_rows[k, 1, pl.ds(r, PARTS, stride=size), :].astype(jnp.bfloat16)
         send_lines(k)
-        if 0 < k <= FORWARDED:
-            forward(k - 1)
     for axis, (ref, ref_diag, _, _) in enumerate(axes):
         wait_bytes(ref_diag.at[:LINE - 1], r2d.at[axis])
-        wait_bytes(ref.at[0, :FORWARDED], rf.at[axis])
-        for k in range(FORWARDED, len(CHUNKS)):
-            wait_bytes(ref.at[:LINE - 1, CHUNKS[k][0], :, lanes_of(k)], r2.at[k, axis])
+        wait_bytes(ref.at[:LINE - 1], r2.at[axis])
 
     size = LINE * GROUP
     v_mat, v_end = v_all[...].reshape(size, DEPTH), v_diag[...].reshape(size, LANES)
@@ -243,11 +231,9 @@
 
     for k, (c, _, _) in enumerate(CHUNKS):
         wait_bytes(recv1.at[c, :PARTS - 1, rows_of(k)[1]], s1.at[k])
-        for axis in range(2):
-            wait_bytes(v_all.at[:2 if k < FORWARDED else LINE - 1, c, :, lanes_of(k)], s2.at[k, axis])
     wait_bytes(recv1_diag.at[:PARTS - 1], s1d)
     for axis in range(2):
-        wait_bytes(v_all.at[0, :FORWARDED], sf.at[axis])
+        wait_bytes(v_all.at[:LINE - 1], s2.at[axis])
         wait_bytes(v_diag.at[:LINE - 1], s2d.at[axis])
     for swap in swaps:
         swap.wait_send()
@@ -273,7 +259,7 @@
             pltpu.VMEM((COUNT, PARTS, 2 * ROWS, LANES), bf16),
             pltpu.VMEM((2 * COUNT, LANES), bf16),
             pltpu.VMEM((PARTS, 2 * COUNT, LANES), bf16),
-            pltpu.VMEM((len(CHUNKS), 2, PARTS * ROWS, LANES), f32),
+            pltpu.VMEM((len(CHUNKS), 2, PARTS * ROWS // 2, LANES), f32),
             pltpu.VMEM((PARTS * 2 * COUNT, LANES), f32),
             pltpu.VMEM((LINE, COUNT, PARTS, DEPTH), bf16),
             pltpu.VMEM((LINE, COUNT, PARTS, DEPTH), bf16),
@@ -287,13 +273,13 @@
             pltpu.VMEM((LINE * COUNT, size), f32),
             dma((COUNT + 2,)),
             dma((len(CHUNKS),)), dma((len(CHUNKS),)), dma, dma,
-            dma((len(CHUNKS), 2)), dma((len(CHUNKS), 2)), dma((2,)), dma((2,)), dma((2,)), dma((2,)),
+            dma((2,)), dma((2,)), dma((2,)), dma((2,)),
             dma((RING,)), dma((RING,)), dma, dma,
             dma((len(CHUNKS),)),
         ],
-        compiler_params=pltpu.CompilerParams(collective_id=0, has_side_effects=True),
+        compiler_params=pltpu.CompilerParams(collective_id=0, has_side_effects=True, vmem_limit_bytes=32 << 20),
         name="schur",
-    )(constraint_mats, primal_matrix, inverse_dual_iterate)
+    )(*(pltpu.with_memory_space_constraint(m, pltpu.HBM) for m in (constraint_mats, primal_matrix, inverse_dual_iterate)))
 
 
 def solution(mesh):

time: 42.9 us -> 40 us (0.932)
  Pallas kernels: 41.3 us -> 39.3 us
  local copies, waits for them, and re-layouts: 1.32 us -> 0.61 us
    pallas_call x1, Pallas kernels: 41.3 us -> 39.3 us  [body(): pl.pallas_call(kernel, out_shape=jax.ShapeDtypeStruct((COUNT, 1024), f32)...]
    unnamed x1, local copies, waits for them, and re-layouts: 1.32 us -> 0.61 us
where the time goes in v6:
time: 40 us; the launch traced here: 39.9 us
  Pallas kernels  39.3 us (98%)
  local copies, waits for them, and re-layouts  0.61 us (2%)
    pallas_call x1, Pallas kernels, body(): pl.pallas_call(kernel, out_shape=jax.ShapeDtypeStruct((COUNT, 1024), f32)...  39.3 us

profile of v6, /device:TPU:1, one launch (start us, length us, event | category | flops | bytes accessed | tf_op | source)
XLA Modules:
  0.0 39.9 jit_solution(8118125288282181979)
XLA Ops:
  0.0 39.3 %schur.1 = f32[4,1024]{1,0:T(4,128)S(1)} custom-call(bf16[4,256,256]{2,1,0:T(8,128)(2,1)} %a_hbm.1, bf16[256,256]{1,0:T(8,128)(2,1)} %x_hbm.1, bf16[256,256]{1,0:T(8,128)(2,1)} %z_hbm.1), custom_call_target="tpu_custom_call" | custom-call | tf_op jit(solution)/shard_map/schur/pallas_call | solution.py:249
  39.3 0.6 %copy.5 = f32[4,1024]{1,0:T(4,128)} copy(f32[4,1024]{1,0:T(4,128)S(1)} %schur.1) | data formatting | bytes 32768

commit v7 on v6

v7 whole, which is shorter than its diff:
```python
import jax
import jax.numpy as jnp
from jax import lax
from jax.experimental import pallas as pl
from jax.experimental.pallas import tpu as pltpu
from jax.sharding import PartitionSpec as P

RING = 8
LINE = 4
COUNT = 4
LANES = 128
ROWS = 32
UNIT = 8
DEPTH = ROWS * LANES
FAR_FIRST = (4, 3, 5, 2, 6, 1, 7, 0)
UNITS = tuple((pair, quarter) for pair in range(2) for quarter in range(4))
LAST = len(UNITS) - 1
ORDER = [("a", 0), ("a", 1)] + [w for u in range(LAST - 1) for w in (("v", u), ("a", u + 2))] + [("v", LAST - 1), ("v", LAST)]
SLOT = {what: 16 * i for i, what in enumerate(ORDER)}
MESSAGES = tuple([(0, 3)] + [(2 * k + 1, 2 * k + 3) for k in range(1, LAST)] + [(2 * LAST + 1, 2 * LAST + 2)])
DIAG_MESSAGE = 4


def dot(a, b):
    return lax.dot_general(a, b, (((1,), (0,)), ((), ())), preferred_element_type=jnp.float32)


def dot_nt(a, b):
    return lax.dot_general(a, b, (((1,), (1,)), ((), ())), preferred_element_type=jnp.float32)


def pick_lanes(value, pick):
    high = value.astype(jnp.bfloat16)
    rest = value - high.astype(jnp.float32)
    mid = rest.astype(jnp.bfloat16)
    low = (rest - mid.astype(jnp.float32)).astype(jnp.bfloat16)
    return dot(high, pick) + dot(mid, pick) + dot(low, pick)


def kernel(a_hbm, x_hbm, z_hbm, out_ref, mats, primal_ref, dual_ref, send1, recv1, send1_diag, recv1_diag, wide_rows,
           diag_rows, v_all, a_all, v_diag, a_diag, partial, send3, recv3, joined,
           load, s1, r1, s1d, r1d, s2, r2v, r2a, s2d, r2d, sc, rc, s3, r3, own_sem):
    wide, narrow = lax.axis_index("wide"), lax.axis_index("narrow")
    z_hi = lax.div(narrow, 2)
    core = narrow - 2 * z_hi
    z_lo = lax.div(wide, 16)
    plane = wide - 16 * z_lo
    x = lax.div(plane, 4)
    y = plane - 4 * x
    z = z_hi * 4 + z_lo

    def wrap(value, size):
        return jnp.where(value >= size, value - size, value)

    column, same_core = [], []
    for dz in FAR_FIRST:
        z_at = wrap(z + dz, RING)
        hi = jnp.where(z_at >= 4, 1, 0)
        lo = z_at - 4 * hi
        if dz:
            column.append((z_at, {"wide": lo * 16 + plane, "narrow": 2 * hi + core}))
        same_core.append((z_at, lo * 16 + x * 4, 2 * hi + core))
    line_x, line_y = [], []
    for k in (2, 1, 3):
        x_at, y_at = wrap(x + k, LINE), wrap(y + k, LINE)
        line_x.append((x_at, {"wide": z_lo * 16 + x_at * 4 + y, "narrow": narrow}))
        line_y.append((y_at, {"wide": wide - y + y_at, "narrow": narrow}))
    sibling_core = {"wide": wide, "narrow": 2 * z_hi + 1 - core}

    barrier = pltpu.get_barrier_semaphore()
    greeted = [peer for _, peer in column + line_x + line_y] + [sibling_core]
    for peer in greeted:
        pl.semaphore_signal(barrier, inc=1, device_id=peer)

    loads = [pltpu.make_async_copy(x_hbm, primal_ref, load.at[4]), pltpu.make_async_copy(z_hbm, dual_ref, load.at[5])]
    for c in range(COUNT):
        loads.append(pltpu.make_async_copy(a_hbm.at[c], mats.at[c], load.at[c]))
    for copy in loads:
        copy.start()

    def remote(src, dst, send_sem, recv_sem, peer):
        return pltpu.make_async_remote_copy(
            src_ref=src, dst_ref=dst, send_sem=send_sem, recv_sem=recv_sem, device_id=peer
        )

    def wait_bytes(like, sem):
        pltpu.make_async_copy(like, like, sem).wait()

    def rows_of(k):
        first, end = MESSAGES[k]
        return slice(16 * first, 16 * end)

    def own1(k):
        return pltpu.make_async_copy(send1.at[z, rows_of(k)], recv1.at[z, rows_of(k)], own_sem.at[k])

    def send_column(k):
        for to, peer in column:
            remote(send1.at[to, rows_of(k)], recv1.at[z, rows_of(k)], s1.at[k], r1.at[k], peer).start()
        own1(k).start()

    def store_units(kind, c, fold):
        for d in range(RING):
            for quarter in range(4):
                at = d % 4 * ROWS + quarter * UNIT
                slot = SLOT[kind, c // 2 * 4 + quarter] + c % 2 * UNIT
                send1[d, slot:slot + UNIT, :] = fold[d // 4][at:at + UNIT]

    row = lax.broadcasted_iota(jnp.int32, (LANES, LANES), 0)
    col = lax.broadcasted_iota(jnp.int32, (LANES, LANES), 1)
    loads[0].wait()
    loads[1].wait()
    primal, dual = primal_ref[...], dual_ref[...]
    diag_a, diag_v = [], []
    for c in range(COUNT):
        loads[2 + c].wait()
        mat = mats[c]
        mat32 = mat.astype(jnp.float32)
        a_up, a_low = mat32[:LANES, :LANES], mat32[LANES:, LANES:]
        store_units("a", c, [mat[:LANES, LANES:], jnp.where(row <= col, a_up, a_low).astype(jnp.bfloat16)])
        diag_a.append(jnp.sum(jnp.where(row == col, a_low, 0.0), axis=0, keepdims=True))
    for c in range(COUNT):
        mat = mats[c]
        left = dot(primal, mat).astype(jnp.bfloat16)
        top = dot(left[:LANES], dual) + dot_nt(dual[:LANES], left)
        low = dot(left[LANES:], dual[:, LANES:]) + dot_nt(dual[LANES:], left[LANES:])
        corner = jnp.where(row < col, top[:, :LANES], jnp.where(row == col, 0.5 * top[:, :LANES], low))
        store_units("v", c, [top[:, LANES:].astype(jnp.bfloat16), corner.astype(jnp.bfloat16)])
        diag_v.append(jnp.sum(jnp.where(row == col, low, 0.0), axis=0, keepdims=True) * (0.5 / RING))
        if c == 1:
            pl.semaphore_wait(barrier, len(greeted))
            for k in range(DIAG_MESSAGE):
                send_column(k)
    send1_diag[...] = jnp.concatenate(diag_a + diag_v, axis=0).astype(jnp.bfloat16)
    for _, peer in column:
        remote(send1_diag, recv1_diag.at[z], s1d, r1d, peer).start()
    for k in range(DIAG_MESSAGE, len(MESSAGES)):
        send_column(k)
    recv1_diag[z] = send1_diag[...]

    def block(kind, u, who):
        pair, quarter = UNITS[u]
        lanes = slice(quarter * UNIT * LANES, (quarter + 1) * UNIT * LANES)
        return v_all.at[who, pair, :, lanes] if kind == "v" else a_all.at[core, who, pair, :, lanes]

    def pass_on(u):
        wait_bytes(block("a", u, slice(0, LINE - 1)), r2a.at[u])
        whole = block("a", u, slice(None))
        remote(whole, whole, sc, rc, sibling_core).start()

    for k, (first, end) in enumerate(MESSAGES):
        own1(k).wait()
        wait_bytes(recv1.at[:RING - 1, rows_of(k)], r1.at[k])
        for kind, u in ORDER[first:end]:
            slot = SLOT[kind, u]
            for s in range(RING):
                wide_rows[slot // 16, 16 * s:16 * (s + 1), :] = recv1[s, slot:slot + 16, :].astype(jnp.float32)
            to = block(kind, u, y if kind == "v" else x)
            for r in range(UNIT):
                both = [wide_rows[slot // 16, pl.ds(half * UNIT + r, RING, stride=16), :] for half in range(2)]
                to[:, r * LANES:(r + 1) * LANES] = jnp.concatenate(both, axis=0).astype(jnp.bfloat16)
            for _, peer in (line_y if kind == "v" else line_x):
                remote(to, to, s2.at[0 if kind == "v" else 1], r2v if kind == "v" else r2a.at[u], peer).start()
        if k == DIAG_MESSAGE:
            wait_bytes(recv1_diag.at[:RING - 1], r1d)
            for s in range(RING):
                diag_rows[pl.ds(2 * COUNT * s, 2 * COUNT), :] = recv1_diag[s].astype(jnp.float32)
            ends = [diag_rows[pl.ds(i, RING, stride=2 * COUNT), :] for i in range(2 * COUNT)]
            a_diag[core, x] = jnp.concatenate(ends[:COUNT], axis=0).astype(jnp.bfloat16)
            v_diag[y] = jnp.concatenate(ends[COUNT:], axis=0).astype(jnp.bfloat16)
            for axis, (at, line) in enumerate(((v_diag.at[y], line_y), (a_diag.at[core, x], line_x))):
                for _, peer in line:
                    remote(at, at, s2d.at[axis], r2d.at[axis], peer).start()
        if k >= 2:
            pass_on(k - 2)
    wait_bytes(a_diag.at[0, :LINE - 1], r2d.at[1])
    remote(a_diag.at[core], a_diag.at[core], s2d.at[2], r2d.at[2], sibling_core).start()
    pass_on(LAST - 1)
    pass_on(LAST)
    wait_bytes(v_diag.at[:LINE - 1], r2d.at[0])
    wait_bytes(v_all.at[:LINE - 1], r2v)
    wait_bytes(a_diag.at[0], r2d.at[2])
    wait_bytes(a_all.at[0], rc)

    rows, size = LINE * COUNT * RING, 2 * LINE * COUNT * RING
    product = dot_nt(v_all[...].reshape(rows, DEPTH), a_all[...].reshape(size, DEPTH)) + dot_nt(
        v_diag[...].reshape(rows, LANES), a_diag[...].reshape(size, LANES)
    )
    for h in range(2):
        partial[h] = product[:, LANES * h:LANES * (h + 1)]
    own = z * LINE + y
    for i, (z_at, base, narrow_at) in enumerate(same_core):
        for h in range(2):
            piece = partial[h, pl.ds(z_at, LINE * COUNT, stride=RING), :]
            for k in range(LINE):
                send3[z_at * LINE + k, :, LANES * h:LANES * (h + 1)] = piece[COUNT * k:COUNT * (k + 1)]
        for y_at in [y_at for y_at, _ in line_y] + ([y] if i < RING - 1 else []):
            peer = {"wide": base + y_at, "narrow": narrow_at}
            remote(send3.at[z_at * LINE + y_at], recv3.at[own], s3, r3, peer).start()
    recv3[own] = send3[own]

    lane_from = lax.broadcasted_iota(jnp.int32, (size, size), 0)
    lane_to = lax.broadcasted_iota(jnp.int32, (size, size), 1)
    digit = lambda place: lax.rem(lax.div(lane_to, place), 4)
    odd = lax.rem(digit(64), 2)
    first = odd * 128 + digit(16) * 32 + digit(1) * 8 + lax.div(digit(64), 2) * 4 + digit(4)
    second = digit(4) * 64 + digit(16) * 16 + digit(64) * 4 + digit(1)
    pick1 = jnp.where(lane_from == first, 1.0, 0.0).astype(jnp.bfloat16)
    pick2 = jnp.where(lane_from == second, 1.0, 0.0).astype(jnp.bfloat16)

    wait_bytes(recv3.at[:RING * LINE - 1], r3)
    totals = []
    for k in range(LINE):
        total = recv3[k]
        for z_from in range(1, RING):
            total = total + recv3[z_from * LINE + k]
        totals.append(total)
    grouped = pick_lanes(jnp.concatenate(totals, axis=0), pick1)
    for k in range(LINE):
        for n in range(LINE):
            joined[COUNT * n:COUNT * (n + 1), 64 * k:64 * (k + 1)] = grouped[
                COUNT * k:COUNT * (k + 1), 64 * n:64 * (n + 1)
            ]
    ordered = pick_lanes(joined[...], pick2)
    for n in range(LINE):
        out_ref[:, size * n:size * (n + 1)] = ordered[COUNT * n:COUNT * (n + 1)]

    for k in range(len(MESSAGES)):
        wait_bytes(recv1.at[:RING - 1, rows_of(k)], s1.at[k])
    wait_bytes(recv1_diag.at[:RING - 1], s1d)
    wait_bytes(v_all.at[:LINE - 1], s2.at[0])
    wait_bytes(a_all.at[0, :LINE - 1], s2.at[1])
    wait_bytes(v_diag.at[:LINE - 1], s2d.at[0])
    wait_bytes(a_diag.at[0, :LINE - 1], s2d.at[1])
    wait_bytes(a_diag.at[0], s2d.at[2])
    wait_bytes(a_all.at[0], sc)
    wait_bytes(recv3.at[:RING * LINE - 1], s3)


def body(constraint_mats, primal_matrix, inverse_dual_iterate):
    hbm = pl.BlockSpec(memory_space=pltpu.HBM)
    dma = pltpu.SemaphoreType.DMA
    bf16, f32 = jnp.bfloat16, jnp.float32
    order = 2 * LANES
    rows, size = LINE * COUNT * RING, 2 * LINE * COUNT * RING
    return pl.pallas_call(
        kernel,
        out_shape=jax.ShapeDtypeStruct((COUNT, 1024), f32),
        in_specs=[hbm] * 3,
        out_specs=pl.BlockSpec(memory_space=pltpu.VMEM),
        scratch_shapes=[
            pltpu.VMEM((COUNT, order, order), bf16),
            pltpu.VMEM((order, order), bf16),
            pltpu.VMEM((order, order), bf16),
            pltpu.VMEM((RING, 16 * len(ORDER), LANES), bf16),
            pltpu.VMEM((RING, 16 * len(ORDER), LANES), bf16),
            pltpu.VMEM((2 * COUNT, LANES), bf16),
            pltpu.VMEM((RING, 2 * COUNT, LANES), bf16),
            pltpu.VMEM((len(ORDER), RING * 16, LANES), f32),
            pltpu.VMEM((RING * 2 * COUNT, LANES), f32),
            pltpu.VMEM((LINE, 2, 16, DEPTH), bf16),
            pltpu.VMEM((2, LINE, 2, 16, DEPTH), bf16),
            pltpu.VMEM((LINE, COUNT * RING, LANES), bf16),
            pltpu.VMEM((2, LINE, COUNT * RING, LANES), bf16),
            pltpu.VMEM((2, rows, LANES), f32),
            pltpu.VMEM((RING * LINE, COUNT, size), f32),
            pltpu.VMEM((RING * LINE, COUNT, size), f32),
            pltpu.VMEM((LINE * COUNT, size), f32),
            dma((COUNT + 2,)),
            dma((len(MESSAGES),)), dma((len(MESSAGES),)), dma, dma,
            dma((2,)), dma, dma((len(UNITS),)), dma((3,)), dma((3,)), dma, dma,
            dma, dma,
            dma((len(MESSAGES),)),
        ],
        compiler_params=pltpu.CompilerParams(collective_id=0, has_side_effects=True, vmem_limit_bytes=32 << 20),
        name="schur",
    )(*(pltpu.with_memory_space_constraint(m, pltpu.HBM) for m in (constraint_mats, primal_matrix, inverse_dual_iterate)))


def solution(mesh):
    in_specs = (P(("narrow", "wide"), None, None), P(), P())
    out_specs = P(("narrow", "wide"), None)
    return jax.shard_map(body, mesh=mesh, in_specs=in_specs, out_specs=out_specs, check_vma=False)
```

time: 40 us -> 38.8 us (0.970)
  Pallas kernels: 39.3 us -> 38.1 us
    pallas_call x1, Pallas kernels: 39.3 us -> 38.1 us  [body(): pl.pallas_call(kernel, out_shape=jax.ShapeDtypeStruct((COUNT, 1024), f32)...]
where the time goes in v7:
time: 38.8 us; the launch traced here: 38.7 us
  Pallas kernels  38.1 us (98%)
  local copies, waits for them, and re-layouts  0.61 us (2%)
    pallas_call x1, Pallas kernels, body(): pl.pallas_call(kernel, out_shape=jax.ShapeDtypeStruct((COUNT, 1024), f32)...  38.1 us

profile of v7, /device:TPU:1, one launch (start us, length us, event | category | flops | bytes accessed | tf_op | source)
XLA Modules:
  0.0 38.7 jit_solution(878591091606547290)
XLA Ops:
  0.0 38.1 %schur.1 = f32[4,1024]{1,0:T(4,128)S(1)} custom-call(bf16[4,256,256]{2,1,0:T(8,128)(2,1)} %a_hbm.1, bf16[256,256]{1,0:T(8,128)(2,1)} %x_hbm.1, bf16[256,256]{1,0:T(8,128)(2,1)} %z_hbm.1), custom_call_target="tpu_custom_call" | custom-call | tf_op jit(solution)/shard_map/schur/pallas_call | solution.py:245
  38.1 0.6 %copy.5 = f32[4,1024]{1,0:T(4,128)} copy(f32[4,1024]{1,0:T(4,128)S(1)} %schur.1) | data formatting | bytes 32768

commit v8 on v7

--- a/solution.py
+++ b/solution.py
@@ -17,8 +17,8 @@
 LAST = len(UNITS) - 1
 ORDER = [("a", 0), ("a", 1)] + [w for u in range(LAST - 1) for w in (("v", u), ("a", u + 2))] + [("v", LAST - 1), ("v", LAST)]
 SLOT = {what: 16 * i for i, what in enumerate(ORDER)}
-MESSAGES = tuple([(0, 3)] + [(2 * k + 1, 2 * k + 3) for k in range(1, LAST)] + [(2 * LAST + 1, 2 * LAST + 2)])
-DIAG_MESSAGE = 4
+MESSAGES = tuple([(0, 2), (2, 3)] + [(2 * k + 1, 2 * k + 3) for k in range(1, LAST)] + [(2 * LAST + 1, 2 * LAST + 2)])
+DIAG_MESSAGE = 5
 
 
 def dot(a, b):
@@ -34,11 +34,13 @@
     rest = value - high.astype(jnp.float32)
     mid = rest.astype(jnp.bfloat16)
     low = (rest - mid.astype(jnp.float32)).astype(jnp.bfloat16)
-    return dot(high, pick) + dot(mid, pick) + dot(low, pick)
+    count = value.shape[0]
+    parts = dot(jnp.concatenate([high, mid, low], axis=0), pick)
+    return parts[:count] + parts[count:2 * count] + parts[2 * count:]
 
 
 def kernel(a_hbm, x_hbm, z_hbm, out_ref, mats, primal_ref, dual_ref, send1, recv1, send1_diag, recv1_diag, wide_rows,
-           diag_rows, v_all, a_all, v_diag, a_diag, partial, send3, recv3, joined,
+           diag_rows, v_all, a_all, v_diag, a_diag, partial, send3, recv3,
            load, s1, r1, s1d, r1d, s2, r2v, r2a, s2d, r2d, sc, rc, s3, r3, own_sem):
     wide, narrow = lax.axis_index("wide"), lax.axis_index("narrow")
     z_hi = lax.div(narrow, 2)
@@ -75,8 +77,8 @@
     loads = [pltpu.make_async_copy(x_hbm, primal_ref, load.at[4]), pltpu.make_async_copy(z_hbm, dual_ref, load.at[5])]
     for c in range(COUNT):
         loads.append(pltpu.make_async_copy(a_hbm.at[c], mats.at[c], load.at[c]))
-    for copy in loads:
-        copy.start()
+    for i in (2, 3, 0, 1, 4, 5):
+        loads[i].start()
 
     def remote(src, dst, send_sem, recv_sem, peer):
         return pltpu.make_async_remote_copy(
@@ -107,9 +109,6 @@
 
     row = lax.broadcasted_iota(jnp.int32, (LANES, LANES), 0)
     col = lax.broadcasted_iota(jnp.int32, (LANES, LANES), 1)
-    loads[0].wait()
-    loads[1].wait()
-    primal, dual = primal_ref[...], dual_ref[...]
     diag_a, diag_v = [], []
     for c in range(COUNT):
         loads[2 + c].wait()
@@ -118,6 +117,12 @@
         a_up, a_low = mat32[:LANES, :LANES], mat32[LANES:, LANES:]
         store_units("a", c, [mat[:LANES, LANES:], jnp.where(row <= col, a_up, a_low).astype(jnp.bfloat16)])
         diag_a.append(jnp.sum(jnp.where(row == col, a_low, 0.0), axis=0, keepdims=True))
+        if c == 1:
+            pl.semaphore_wait(barrier, len(greeted))
+            send_column(0)
+    loads[0].wait()
+    loads[1].wait()
+    primal, dual = primal_ref[...], dual_ref[...]
     for c in range(COUNT):
         mat = mats[c]
         left = dot(primal, mat).astype(jnp.bfloat16)
@@ -127,8 +132,7 @@
         store_units("v", c, [top[:, LANES:].astype(jnp.bfloat16), corner.astype(jnp.bfloat16)])
         diag_v.append(jnp.sum(jnp.where(row == col, low, 0.0), axis=0, keepdims=True) * (0.5 / RING))
         if c == 1:
-            pl.semaphore_wait(barrier, len(greeted))
-            for k in range(DIAG_MESSAGE):
+            for k in range(1, DIAG_MESSAGE):
                 send_column(k)
     send1_diag[...] = jnp.concatenate(diag_a + diag_v, axis=0).astype(jnp.bfloat16)
     for _, peer in column:
@@ -145,7 +149,7 @@
     def pass_on(u):
         wait_bytes(block("a", u, slice(0, LINE - 1)), r2a.at[u])
         whole = block("a", u, slice(None))
-        remote(whole, whole, sc, rc, sibling_core).start()
+        remote(whole, whole, sc, rc.at[u // LAST], sibling_core).start()
 
     for k, (first, end) in enumerate(MESSAGES):
         own1(k).wait()
@@ -159,7 +163,7 @@
                 both = [wide_rows[slot // 16, pl.ds(half * UNIT + r, RING, stride=16), :] for half in range(2)]
                 to[:, r * LANES:(r + 1) * LANES] = jnp.concatenate(both, axis=0).astype(jnp.bfloat16)
             for _, peer in (line_y if kind == "v" else line_x):
-                remote(to, to, s2.at[0 if kind == "v" else 1], r2v if kind == "v" else r2a.at[u], peer).start()
+                remote(to, to, s2.at[0 if kind == "v" else 1], r2v.at[u // LAST] if kind == "v" else r2a.at[u], peer).start()
         if k == DIAG_MESSAGE:
             wait_bytes(recv1_diag.at[:RING - 1], r1d)
             for s in range(RING):
@@ -170,21 +174,25 @@
             for axis, (at, line) in enumerate(((v_diag.at[y], line_y), (a_diag.at[core, x], line_x))):
                 for _, peer in line:
                     remote(at, at, s2d.at[axis], r2d.at[axis], peer).start()
-        if k >= 2:
-            pass_on(k - 2)
+        if k >= 3:
+            pass_on(k - 3)
     wait_bytes(a_diag.at[0, :LINE - 1], r2d.at[1])
     remote(a_diag.at[core], a_diag.at[core], s2d.at[2], r2d.at[2], sibling_core).start()
     pass_on(LAST - 1)
     pass_on(LAST)
+
+    rows, size = LINE * COUNT * RING, 2 * LINE * COUNT * RING
     wait_bytes(v_diag.at[:LINE - 1], r2d.at[0])
-    wait_bytes(v_all.at[:LINE - 1], r2v)
     wait_bytes(a_diag.at[0], r2d.at[2])
-    wait_bytes(a_all.at[0], rc)
-
-    rows, size = LINE * COUNT * RING, 2 * LINE * COUNT * RING
-    product = dot_nt(v_all[...].reshape(rows, DEPTH), a_all[...].reshape(size, DEPTH)) + dot_nt(
-        v_diag[...].reshape(rows, LANES), a_diag[...].reshape(size, LANES)
-    )
+    product = dot_nt(v_diag[...].reshape(rows, LANES), a_diag[...].reshape(size, LANES))
+    most = LAST % 4 * UNIT * LANES
+    seven = DEPTH * LAST // len(UNITS)
+    wait_bytes(v_all.at[:LINE - 1, :, :, :seven], r2v.at[0])
+    wait_bytes(a_all.at[0, :, :, :, :seven], rc.at[0])
+    product += dot_nt(v_all[:, :, :, :most].reshape(rows, most), a_all[:, :, :, :, :most].reshape(size, most))
+    wait_bytes(v_all.at[:LINE - 1, 0, :, most:], r2v.at[1])
+    wait_bytes(a_all.at[0, :, 0, :, most:], rc.at[1])
+    product += dot_nt(v_all[:, :, :, most:].reshape(rows, DEPTH - most), a_all[:, :, :, :, most:].reshape(size, DEPTH - most))
     for h in range(2):
         partial[h] = product[:, LANES * h:LANES * (h + 1)]
     own = z * LINE + y
@@ -198,14 +206,11 @@
             remote(send3.at[z_at * LINE + y_at], recv3.at[own], s3, r3, peer).start()
     recv3[own] = send3[own]
 
-    lane_from = lax.broadcasted_iota(jnp.int32, (size, size), 0)
-    lane_to = lax.broadcasted_iota(jnp.int32, (size, size), 1)
-    digit = lambda place: lax.rem(lax.div(lane_to, place), 4)
-    odd = lax.rem(digit(64), 2)
-    first = odd * 128 + digit(16) * 32 + digit(1) * 8 + lax.div(digit(64), 2) * 4 + digit(4)
-    second = digit(4) * 64 + digit(16) * 16 + digit(64) * 4 + digit(1)
-    pick1 = jnp.where(lane_from == first, 1.0, 0.0).astype(jnp.bfloat16)
-    pick2 = jnp.where(lane_from == second, 1.0, 0.0).astype(jnp.bfloat16)
+    lane_from = lax.broadcasted_iota(jnp.int32, (size, 4 * size), 0)
+    lane_to = lax.broadcasted_iota(jnp.int32, (size, 4 * size), 1)
+    digit = lambda place, base=4: lax.rem(lax.div(lane_to, place), base)
+    source = digit(256, 2) * 128 + digit(16) * 32 + digit(1) * 8 + digit(512, 2) * 4 + digit(64)
+    pick = jnp.where((lane_from == source) & (digit(4) == 0), 1.0, 0.0).astype(jnp.bfloat16)
 
     wait_bytes(recv3.at[:RING * LINE - 1], r3)
     totals = []
@@ -214,15 +219,11 @@
         for z_from in range(1, RING):
             total = total + recv3[z_from * LINE + k]
         totals.append(total)
-    grouped = pick_lanes(jnp.concatenate(totals, axis=0), pick1)
-    for k in range(LINE):
-        for n in range(LINE):
-            joined[COUNT * n:COUNT * (n + 1), 64 * k:64 * (k + 1)] = grouped[
-                COUNT * k:COUNT * (k + 1), 64 * n:64 * (n + 1)
-            ]
-    ordered = pick_lanes(joined[...], pick2)
-    for n in range(LINE):
-        out_ref[:, size * n:size * (n + 1)] = ordered[COUNT * n:COUNT * (n + 1)]
+    ordered = pick_lanes(jnp.concatenate(totals, axis=0), pick)
+    result = ordered[:COUNT]
+    for k in range(1, LINE):
+        result = result + pltpu.roll(ordered, COUNT * k, 1)[COUNT * k:COUNT * (k + 1)]
+    out_ref[...] = result
 
     for k in range(len(MESSAGES)):
         wait_bytes(recv1.at[:RING - 1, rows_of(k)], s1.at[k])
@@ -264,10 +265,9 @@
             pltpu.VMEM((2, rows, LANES), f32),
             pltpu.VMEM((RING * LINE, COUNT, size), f32),
             pltpu.VMEM((RING * LINE, COUNT, size), f32),
-            pltpu.VMEM((LINE * COUNT, size), f32),
             dma((COUNT + 2,)),
             dma((len(MESSAGES),)), dma((len(MESSAGES),)), dma, dma,
-            dma((2,)), dma, dma((len(UNITS),)), dma((3,)), dma((3,)), dma, dma,
+            dma((2,)), dma((2,)), dma((len(UNITS),)), dma((3,)), dma((3,)), dma, dma((2,)),
             dma, dma,
             dma((len(MESSAGES),)),
         ],

time: 38.8 us -> 38.1 us (0.982)
  Pallas kernels: 38.1 us -> 37.4 us
    pallas_call x1, Pallas kernels: 38.1 us -> 37.4 us  [body(): pl.pallas_call(kernel, out_shape=jax.ShapeDtypeStruct((COUNT, 1024), f32)...]
where the time goes in v8:
time: 38.1 us; the launch traced here: 38 us
  Pallas kernels  37.4 us (98%)
  local copies, waits for them, and re-layouts  0.61 us (2%)
    pallas_call x1, Pallas kernels, body(): pl.pallas_call(kernel, out_shape=jax.ShapeDtypeStruct((COUNT, 1024), f32)...  37.4 us

profile of v8, /device:TPU:1, one launch (start us, length us, event | category | flops | bytes accessed | tf_op | source)
XLA Modules:
  0.0 38.0 jit_solution(16816421457089901124)
XLA Ops:
  0.0 37.4 %schur.1 = f32[4,1024]{1,0:T(4,128)S(1)} custom-call(bf16[4,256,256]{2,1,0:T(8,128)(2,1)} %a_hbm.1, bf16[256,256]{1,0:T(8,128)(2,1)} %x_hbm.1, bf16[256,256]{1,0:T(8,128)(2,1)} %z_hbm.1), custom_call_target="tpu_custom_call" | custom-call | tf_op jit(solution)/shard_map/schur/pallas_call | solution.py:246
  37.4 0.6 %copy.5 = f32[4,1024]{1,0:T(4,128)} copy(f32[4,1024]{1,0:T(4,128)S(1)} %schur.1) | data formatting | bytes 32768

commit v9 on v8

--- a/solution.py
+++ b/solution.py
@@ -12,12 +12,12 @@
 ROWS = 32
 UNIT = 8
 DEPTH = ROWS * LANES
-FAR_FIRST = (4, 3, 5, 2, 6, 1, 7, 0)
+FAR_FIRST = (4, 3, 5, 2, 6, 1, 7)
 UNITS = tuple((pair, quarter) for pair in range(2) for quarter in range(4))
 LAST = len(UNITS) - 1
-ORDER = [("a", 0), ("a", 1)] + [w for u in range(LAST - 1) for w in (("v", u), ("a", u + 2))] + [("v", LAST - 1), ("v", LAST)]
+ORDER = [("a", 0), ("a", 1), ("a", 2)] + [w for u in range(LAST - 2) for w in (("v", u), ("a", u + 3))] + [("v", LAST - 2), ("v", LAST - 1), ("v", LAST)]
 SLOT = {what: 16 * i for i, what in enumerate(ORDER)}
-MESSAGES = tuple([(0, 2), (2, 3)] + [(2 * k + 1, 2 * k + 3) for k in range(1, LAST)] + [(2 * LAST + 1, 2 * LAST + 2)])
+MESSAGES = ((0, 2), (2, 4), (4, 6), (6, 8), (8, 10), (10, 12), (12, 14), (14, 15), (15, 16))
 DIAG_MESSAGE = 5
 
 
@@ -54,14 +54,12 @@
     def wrap(value, size):
         return jnp.where(value >= size, value - size, value)
 
-    column, same_core = [], []
+    column = []
     for dz in FAR_FIRST:
         z_at = wrap(z + dz, RING)
         hi = jnp.where(z_at >= 4, 1, 0)
         lo = z_at - 4 * hi
-        if dz:
-            column.append((z_at, {"wide": lo * 16 + plane, "narrow": 2 * hi + core}))
-        same_core.append((z_at, lo * 16 + x * 4, 2 * hi + core))
+        column.append((z_at, {"wide": lo * 16 + plane, "narrow": 2 * hi + core}))
     line_x, line_y = [], []
     for k in (2, 1, 3):
         x_at, y_at = wrap(x + k, LINE), wrap(y + k, LINE)
@@ -196,21 +194,39 @@
     for h in range(2):
         partial[h] = product[:, LANES * h:LANES * (h + 1)]
     own = z * LINE + y
-    for i, (z_at, base, narrow_at) in enumerate(same_core):
+    for z_to in range(RING):
         for h in range(2):
-            piece = partial[h, pl.ds(z_at, LINE * COUNT, stride=RING), :]
+            piece = partial[h, pl.ds(z_to, LINE * COUNT, stride=RING), :]
             for k in range(LINE):
-                send3[z_at * LINE + k, :, LANES * h:LANES * (h + 1)] = piece[COUNT * k:COUNT * (k + 1)]
-        for y_at in [y_at for y_at, _ in line_y] + ([y] if i < RING - 1 else []):
-            peer = {"wide": base + y_at, "narrow": narrow_at}
-            remote(send3.at[z_at * LINE + y_at], recv3.at[own], s3, r3, peer).start()
+                send3[z_to * LINE + k, :, LANES * h:LANES * (h + 1)] = piece[COUNT * k:COUNT * (k + 1)]
+
+    for to in [0, 8, 4, 12] + [k for k in range(32) if k not in (0, 8, 4, 12)]:
+        z_to, y_to = divmod(to, LINE)
+
+        @pl.when(own != to)
+        def _():
+            peer = {"wide": z_to % 4 * 16 + x * 4 + y_to, "narrow": z_to // 4 * 2 + core}
+            remote(send3.at[to], recv3.at[own], s3, r3, peer).start()
+
     recv3[own] = send3[own]
 
     lane_from = lax.broadcasted_iota(jnp.int32, (size, 4 * size), 0)
-    lane_to = lax.broadcasted_iota(jnp.int32, (size, 4 * size), 1)
+    lane_to = lax.broadcasted_iota(jnp.int32, (1, 4 * size), 1)
     digit = lambda place, base=4: lax.rem(lax.div(lane_to, place), base)
     source = digit(256, 2) * 128 + digit(16) * 32 + digit(1) * 8 + digit(512, 2) * 4 + digit(64)
-    pick = jnp.where((lane_from == source) & (digit(4) == 0), 1.0, 0.0).astype(jnp.bfloat16)
+    source = jnp.where(digit(4) == 0, source, -1)
+    pick = jnp.where(lane_from == source, 1.0, 0.0).astype(jnp.bfloat16)
+
+    for k in range(len(MESSAGES)):
+        wait_bytes(recv1.at[:RING - 1, rows_of(k)], s1.at[k])
+    wait_bytes(recv1_diag.at[:RING - 1], s1d)
+    wait_bytes(v_all.at[:LINE - 1], s2.at[0])
+    wait_bytes(a_all.at[0, :LINE - 1], s2.at[1])
+    wait_bytes(v_diag.at[:LINE - 1], s2d.at[0])
+    wait_bytes(a_diag.at[0, :LINE - 1], s2d.at[1])
+    wait_bytes(a_diag.at[0], s2d.at[2])
+    wait_bytes(a_all.at[0], sc)
+    wait_bytes(recv3.at[:RING * LINE - 1], s3)
 
     wait_bytes(recv3.at[:RING * LINE - 1], r3)
     totals = []
@@ -224,17 +240,6 @@
     for k in range(1, LINE):
         result = result + pltpu.roll(ordered, COUNT * k, 1)[COUNT * k:COUNT * (k + 1)]
     out_ref[...] = result
-
-    for k in range(len(MESSAGES)):
-        wait_bytes(recv1.at[:RING - 1, rows_of(k)], s1.at[k])
-    wait_bytes(recv1_diag.at[:RING - 1], s1d)
-    wait_bytes(v_all.at[:LINE - 1], s2.at[0])
-    wait_bytes(a_all.at[0, :LINE - 1], s2.at[1])
-    wait_bytes(v_diag.at[:LINE - 1], s2d.at[0])
-    wait_bytes(a_diag.at[0, :LINE - 1], s2d.at[1])
-    wait_bytes(a_diag.at[0], s2d.at[2])
-    wait_bytes(a_all.at[0], sc)
-    wait_bytes(recv3.at[:RING * LINE - 1], s3)
 
 
 def body(constraint_mats, primal_matrix, inverse_dual_iterate):

time: 38.1 us -> 37 us (0.971)
  Pallas kernels: 37.4 us -> 36.3 us
    pallas_call x1, Pallas kernels: 37.4 us -> 36.3 us  [body(): pl.pallas_call(kernel, out_shape=jax.ShapeDtypeStruct((COUNT, 1024), f32)...]
where the time goes in v9:
time: 37 us; the launch traced here: 36.9 us
  Pallas kernels  36.3 us (98%)
  local copies, waits for them, and re-layouts  0.61 us (2%)
    pallas_call x1, Pallas kernels, body(): pl.pallas_call(kernel, out_shape=jax.ShapeDtypeStruct((COUNT, 1024), f32)...  36.3 us

profile of v9, /device:TPU:1, one launch (start us, length us, event | category | flops | bytes accessed | tf_op | source)
XLA Modules:
  0.0 36.9 jit_solution(15851008843474459633)
XLA Ops:
  0.0 36.3 %schur.1 = f32[4,1024]{1,0:T(4,128)S(1)} custom-call(bf16[4,256,256]{2,1,0:T(8,128)(2,1)} %a_hbm.1, bf16[256,256]{1,0:T(8,128)(2,1)} %x_hbm.1, bf16[256,256]{1,0:T(8,128)(2,1)} %z_hbm.1), custom_call_target="tpu_custom_call" | custom-call | tf_op jit(solution)/shard_map/schur/pallas_call | solution.py:251
  36.3 0.6 %copy.5 = f32[4,1024]{1,0:T(4,128)} copy(f32[4,1024]{1,0:T(4,128)S(1)} %schur.1) | data formatting | bytes 32768

commit v10 on v9

--- a/solution.py
+++ b/solution.py
@@ -41,7 +41,7 @@
 
 def kernel(a_hbm, x_hbm, z_hbm, out_ref, mats, primal_ref, dual_ref, send1, recv1, send1_diag, recv1_diag, wide_rows,
            diag_rows, v_all, a_all, v_diag, a_diag, partial, send3, recv3,
-           load, s1, r1, s1d, r1d, s2, r2v, r2a, s2d, r2d, sc, rc, s3, r3, own_sem):
+           load, s1, r1, s1d, r1d, s2, r2v, r2a, s2d, r2d, sc, rc, s3, r3):
     wide, narrow = lax.axis_index("wide"), lax.axis_index("narrow")
     z_hi = lax.div(narrow, 2)
     core = narrow - 2 * z_hi
@@ -72,11 +72,11 @@
     for peer in greeted:
         pl.semaphore_signal(barrier, inc=1, device_id=peer)
 
-    loads = [pltpu.make_async_copy(x_hbm, primal_ref, load.at[4]), pltpu.make_async_copy(z_hbm, dual_ref, load.at[5])]
-    for c in range(COUNT):
-        loads.append(pltpu.make_async_copy(a_hbm.at[c], mats.at[c], load.at[c]))
-    for i in (2, 3, 0, 1, 4, 5):
-        loads[i].start()
+    for pair in range(2):
+        pltpu.make_async_copy(a_hbm.at[2 * pair:2 * pair + 2], mats.at[2 * pair:2 * pair + 2], load.at[pair]).start()
+        if pair == 0:
+            pltpu.make_async_copy(x_hbm, primal_ref, load.at[2]).start()
+            pltpu.make_async_copy(z_hbm, dual_ref, load.at[2]).start()
 
     def remote(src, dst, send_sem, recv_sem, peer):
         return pltpu.make_async_remote_copy(
@@ -91,11 +91,11 @@
         return slice(16 * first, 16 * end)
 
     def own1(k):
-        return pltpu.make_async_copy(send1.at[z, rows_of(k)], recv1.at[z, rows_of(k)], own_sem.at[k])
+        return pltpu.make_async_copy(send1.at[z, rows_of(k)], recv1.at[z, rows_of(k)], r1.at[k])
 
     def send_column(k):
         for to, peer in column:
-            remote(send1.at[to, rows_of(k)], recv1.at[z, rows_of(k)], s1.at[k], r1.at[k], peer).start()
+            remote(send1.at[to, rows_of(k)], recv1.at[z, rows_of(k)], s1, r1.at[k], peer).start()
         own1(k).start()
 
     def store_units(kind, c, fold):
@@ -109,7 +109,8 @@
     col = lax.broadcasted_iota(jnp.int32, (LANES, LANES), 1)
     diag_a, diag_v = [], []
     for c in range(COUNT):
-        loads[2 + c].wait()
+        if c % 2 == 0:
+            wait_bytes(mats.at[:2], load.at[c // 2])
         mat = mats[c]
         mat32 = mat.astype(jnp.float32)
         a_up, a_low = mat32[:LANES, :LANES], mat32[LANES:, LANES:]
@@ -118,8 +119,7 @@
         if c == 1:
             pl.semaphore_wait(barrier, len(greeted))
             send_column(0)
-    loads[0].wait()
-    loads[1].wait()
+    wait_bytes(mats.at[:2], load.at[2])
     primal, dual = primal_ref[...], dual_ref[...]
     for c in range(COUNT):
         mat = mats[c]
@@ -150,8 +150,7 @@
         remote(whole, whole, sc, rc.at[u // LAST], sibling_core).start()
 
     for k, (first, end) in enumerate(MESSAGES):
-        own1(k).wait()
-        wait_bytes(recv1.at[:RING - 1, rows_of(k)], r1.at[k])
+        wait_bytes(recv1.at[:, rows_of(k)], r1.at[k])
         for kind, u in ORDER[first:end]:
             slot = SLOT[kind, u]
             for s in range(RING):
@@ -161,7 +160,7 @@
                 both = [wide_rows[slot // 16, pl.ds(half * UNIT + r, RING, stride=16), :] for half in range(2)]
                 to[:, r * LANES:(r + 1) * LANES] = jnp.concatenate(both, axis=0).astype(jnp.bfloat16)
             for _, peer in (line_y if kind == "v" else line_x):
-                remote(to, to, s2.at[0 if kind == "v" else 1], r2v.at[u // LAST] if kind == "v" else r2a.at[u], peer).start()
+                remote(to, to, s2, r2v.at[u // LAST] if kind == "v" else r2a.at[u], peer).start()
         if k == DIAG_MESSAGE:
             wait_bytes(recv1_diag.at[:RING - 1], r1d)
             for s in range(RING):
@@ -171,11 +170,11 @@
             v_diag[y] = jnp.concatenate(ends[COUNT:], axis=0).astype(jnp.bfloat16)
             for axis, (at, line) in enumerate(((v_diag.at[y], line_y), (a_diag.at[core, x], line_x))):
                 for _, peer in line:
-                    remote(at, at, s2d.at[axis], r2d.at[axis], peer).start()
+                    remote(at, at, s2d.at[0], r2d.at[axis], peer).start()
         if k >= 3:
             pass_on(k - 3)
     wait_bytes(a_diag.at[0, :LINE - 1], r2d.at[1])
-    remote(a_diag.at[core], a_diag.at[core], s2d.at[2], r2d.at[2], sibling_core).start()
+    remote(a_diag.at[core], a_diag.at[core], s2d.at[1], r2d.at[2], sibling_core).start()
     pass_on(LAST - 1)
     pass_on(LAST)
 
@@ -217,14 +216,11 @@
     source = jnp.where(digit(4) == 0, source, -1)
     pick = jnp.where(lane_from == source, 1.0, 0.0).astype(jnp.bfloat16)
 
-    for k in range(len(MESSAGES)):
-        wait_bytes(recv1.at[:RING - 1, rows_of(k)], s1.at[k])
+    wait_bytes(recv1.at[:RING - 1], s1)
     wait_bytes(recv1_diag.at[:RING - 1], s1d)
-    wait_bytes(v_all.at[:LINE - 1], s2.at[0])
-    wait_bytes(a_all.at[0, :LINE - 1], s2.at[1])
-    wait_bytes(v_diag.at[:LINE - 1], s2d.at[0])
-    wait_bytes(a_diag.at[0, :LINE - 1], s2d.at[1])
-    wait_bytes(a_diag.at[0], s2d.at[2])
+    wait_bytes(a_all.at[:, :LINE - 1], s2)
+    wait_bytes(a_diag.at[:, :LINE - 1], s2d.at[0])
+    wait_bytes(a_diag.at[0], s2d.at[1])
     wait_bytes(a_all.at[0], sc)
     wait_bytes(recv3.at[:RING * LINE - 1], s3)
 
@@ -270,11 +266,10 @@
             pltpu.VMEM((2, rows, LANES), f32),
             pltpu.VMEM((RING * LINE, COUNT, size), f32),
             pltpu.VMEM((RING * LINE, COUNT, size), f32),
-            dma((COUNT + 2,)),
-            dma((len(MESSAGES),)), dma((len(MESSAGES),)), dma, dma,
-            dma((2,)), dma((2,)), dma((len(UNITS),)), dma((3,)), dma((3,)), dma, dma((2,)),
+            dma((3,)),
+            dma, dma((len(MESSAGES),)), dma, dma,
+            dma, dma((2,)), dma((len(UNITS),)), dma((2,)), dma((3,)), dma, dma((2,)),
             dma, dma,
-            dma((len(MESSAGES),)),
         ],
         compiler_params=pltpu.CompilerParams(collective_id=0, has_side_effects=True, vmem_limit_bytes=32 << 20),
         name="schur",

time: 37 us -> 36.8 us (level)
  no operation moved by 1% of the time
where the time goes in v10:
time: 36.8 us; the launch traced here: 36.7 us
  Pallas kernels  36.1 us (98%)
  local copies, waits for them, and re-layouts  0.61 us (2%)
    pallas_call x1, Pallas kernels, body(): pl.pallas_call(kernel, out_shape=jax.ShapeDtypeStruct((COUNT, 1024), f32)...  36.1 us

profile of v10, /device:TPU:1, one launch (start us, length us, event | category | flops | bytes accessed | tf_op | source)
XLA Modules:
  0.0 36.7 jit_solution(1571406524743310168)
XLA Ops:
  0.0 36.1 %schur.1 = f32[4,1024]{1,0:T(4,128)S(1)} custom-call(bf16[4,256,256]{2,1,0:T(8,128)(2,1)} %a_hbm.1, bf16[256,256]{1,0:T(8,128)(2,1)} %x_hbm.1, bf16[256,256]{1,0:T(8,128)(2,1)} %z_hbm.1), custom_call_target="tpu_custom_call" | custom-call | tf_op jit(solution)/shard_map/schur/pallas_call | solution.py:247
  36.1 0.6 %copy.5 = f32[4,1024]{1,0:T(4,128)} copy(f32[4,1024]{1,0:T(4,128)S(1)} %schur.1) | data formatting | bytes 32768

commit v11 on v10

--- a/solution.py
+++ b/solution.py
@@ -15,9 +15,9 @@
 FAR_FIRST = (4, 3, 5, 2, 6, 1, 7)
 UNITS = tuple((pair, quarter) for pair in range(2) for quarter in range(4))
 LAST = len(UNITS) - 1
-ORDER = [("a", 0), ("a", 1), ("a", 2)] + [w for u in range(LAST - 2) for w in (("v", u), ("a", u + 3))] + [("v", LAST - 2), ("v", LAST - 1), ("v", LAST)]
+ORDER = [("a", 0), ("a", 1)] + [w for u in range(LAST - 1) for w in (("v", u), ("a", u + 2))] + [("v", LAST - 1), ("v", LAST)]
 SLOT = {what: 16 * i for i, what in enumerate(ORDER)}
-MESSAGES = ((0, 2), (2, 4), (4, 6), (6, 8), (8, 10), (10, 12), (12, 14), (14, 15), (15, 16))
+MESSAGES = ((0, 2), (2, 3), (3, 5), (5, 7), (7, 9), (9, 11), (11, 13), (13, 15), (15, 16))
 DIAG_MESSAGE = 5
 
 
@@ -171,12 +171,12 @@
             for axis, (at, line) in enumerate(((v_diag.at[y], line_y), (a_diag.at[core, x], line_x))):
                 for _, peer in line:
                     remote(at, at, s2d.at[0], r2d.at[axis], peer).start()
-        if k >= 3:
-            pass_on(k - 3)
+        if k >= 4:
+            pass_on(k - 4)
     wait_bytes(a_diag.at[0, :LINE - 1], r2d.at[1])
     remote(a_diag.at[core], a_diag.at[core], s2d.at[1], r2d.at[2], sibling_core).start()
-    pass_on(LAST - 1)
-    pass_on(LAST)
+    for u in range(LAST - 2, LAST + 1):
+        pass_on(u)
 
     rows, size = LINE * COUNT * RING, 2 * LINE * COUNT * RING
     wait_bytes(v_diag.at[:LINE - 1], r2d.at[0])
@@ -234,7 +234,7 @@
     ordered = pick_lanes(jnp.concatenate(totals, axis=0), pick)
     result = ordered[:COUNT]
     for k in range(1, LINE):
-        result = result + pltpu.roll(ordered, COUNT * k, 1)[COUNT * k:COUNT * (k + 1)]
+        result = result + pltpu.roll(ordered[COUNT * k:COUNT * (k + 1)], COUNT * k, 1)
     out_ref[...] = result
 
 

time: 36.8 us -> 36.9 us (level)
  no operation moved by 1% of the time
where the time goes in v11:
time: 36.9 us; the launch traced here: 36.8 us
  Pallas kernels  36.2 us (98%)
  local copies, waits for them, and re-layouts  0.61 us (2%)
    pallas_call x1, Pallas kernels, body(): pl.pallas_call(kernel, out_shape=jax.ShapeDtypeStruct((COUNT, 1024), f32)...  36.2 us

profile of v11, /device:TPU:1, one launch (start us, length us, event | category | flops | bytes accessed | tf_op | source)
XLA Modules:
  0.0 36.8 jit_solution(15260889844979754893)
XLA Ops:
  0.0 36.2 %schur.1 = f32[4,1024]{1,0:T(4,128)S(1)} custom-call(bf16[4,256,256]{2,1,0:T(8,128)(2,1)} %a_hbm.1, bf16[256,256]{1,0:T(8,128)(2,1)} %x_hbm.1, bf16[256,256]{1,0:T(8,128)(2,1)} %z_hbm.1), custom_call_target="tpu_custom_call" | custom-call | tf_op jit(solution)/shard_map/schur/pallas_call | solution.py:247
  36.2 0.6 %copy.5 = f32[4,1024]{1,0:T(4,128)} copy(f32[4,1024]{1,0:T(4,128)S(1)} %schur.1) | data formatting | bytes 32768

commit v12 on v10

--- a/solution.py
+++ b/solution.py
@@ -234,7 +234,7 @@
     ordered = pick_lanes(jnp.concatenate(totals, axis=0), pick)
     result = ordered[:COUNT]
     for k in range(1, LINE):
-        result = result + pltpu.roll(ordered, COUNT * k, 1)[COUNT * k:COUNT * (k + 1)]
+        result = result + pltpu.roll(ordered[COUNT * k:COUNT * (k + 1)], COUNT * k, 1)
     out_ref[...] = result
 
 

time: 36.8 us -> 36.8 us (level)
  no operation moved by 1% of the time
where the time goes in v12:
time: 36.8 us; the launch traced here: 36.7 us
  Pallas kernels  36.1 us (98%)
  local copies, waits for them, and re-layouts  0.61 us (2%)
    pallas_call x1, Pallas kernels, body(): pl.pallas_call(kernel, out_shape=jax.ShapeDtypeStruct((COUNT, 1024), f32)...  36.1 us

profile of v12, /device:TPU:1, one launch (start us, length us, event | category | flops | bytes accessed | tf_op | source)
XLA Modules:
  0.0 36.7 jit_solution(9438822206383639405)
XLA Ops:
  0.0 36.1 %schur.1 = f32[4,1024]{1,0:T(4,128)S(1)} custom-call(bf16[4,256,256]{2,1,0:T(8,128)(2,1)} %a_hbm.1, bf16[256,256]{1,0:T(8,128)(2,1)} %x_hbm.1, bf16[256,256]{1,0:T(8,128)(2,1)} %z_hbm.1), custom_call_target="tpu_custom_call" | custom-call | tf_op jit(solution)/shard_map/schur/pallas_call | solution.py:247
  36.1 0.6 %copy.5 = f32[4,1024]{1,0:T(4,128)} copy(f32[4,1024]{1,0:T(4,128)S(1)} %schur.1) | data formatting | bytes 32768
